TPU v7x, 1024 devices: a whole 8x8x8 slice. The times are simulated.
1024 devices in a mesh: lat: 64 (over z, x_lo, core), lev: 16 (over x_hi, y).
Axes of the slice: x: 8 (x_hi: 2, x_lo: 4; x = x_hi * 4 + x_lo), y: 8, z: 8, core: 2. Of those that a mesh axis runs over, the one named last changes fastest.
Arguments:
- state: float32 [128, 16, 512, 256], P('lev', None, 'lat'), may hold values from -6 to 6
- cour_lat: float32 [128, 512, 256], P('lev', 'lat'), may hold values from -0.25 to 0.25
- cour_lev: float32 [128, 512, 256], P('lev', 'lat'), may hold values from -0.25 to 0.25
- cour_lon: float32 [128, 512, 256], P('lev', 'lat'), may hold values from -0.25 to 0.25
- remap_weight: float32 [128, 128], replicated, may hold values from -0.5 to 0.5
- w_in: bfloat16 [2048, 768], replicated, may hold values from -0.125 to 0.125
- w_out: bfloat16 [768, 2048], replicated, may hold values from -0.21875 to 0.21875
- w_rad_in: bfloat16 [512, 1024], replicated, may hold values from -0.25 to 0.25
- radiative_final_weights: bfloat16 [1024, 128], replicated, may hold values from -0.1875 to 0.1875
- day_list: int32 [64, 16, 128], P('lat', 'lev'), may hold values from 0 to 127, as said below
- day_count: int32 [64, 16], P('lat', 'lev'), may hold values from 0 to 8, as said below
Outputs:
- new_state: float32 [128, 16, 512, 256], P('lev', None, 'lat')
Inputs may be any that keep to these rules, and one draw needn't show every extreme that they name: Each day_list[b, s] is a permutation of 0 to 127. For every even s, groups s and s + 1 cover the two halves (opposite longitudes) of one latitude row, and day_count[b, s] + day_count[b, s + 1] <= 8; band 0 has a group with exactly 8 blocks.
All inputs are finite; a program needn't handle non-finite values.
Results may differ from a plain program's by a relative error of at most 0.0024.
Values may be sent and summed in bfloat16 or wider, within the bound.
No kernel may reach another device: no remote copies, remote signals or barrier semaphores. Data moves between devices by JAX's collectives and lax.ppermute only.
A program may use at most 64 MiB of HBM per device.

v0:
```python
import jax
import jax.numpy as jnp
from jax import lax
from jax.sharding import PartitionSpec as P

RADF = 4
DB = 16


def with_halo(cells, sides, width):
    for axis, dim in sides:
        count = lax.axis_size(axis)
        ends = count - 1
        head = lax.slice_in_dim(cells, 0, width, axis=dim)
        tail = lax.slice_in_dim(cells, cells.shape[dim] - width, cells.shape[dim], axis=dim)
        cells = jnp.concatenate(
            [
                lax.ppermute(tail, axis, [(i, (i + 1) % count) for i in range(ends)]),
                cells,
                lax.ppermute(head, axis, [((i + 1) % count, i) for i in range(ends)]),
            ],
            axis=dim,
        )
    return cells


def advance(tracer, north_rate, sinking_speed, east_rate):
    flux_lat = (
        jnp.maximum(north_rate[:, :, :-1], 0.0) * tracer[:, :, :-1]
        + jnp.minimum(north_rate[:, :, :-1], 0.0) * tracer[:, :, 1:]
    )
    flux_lev = (
        jnp.maximum(sinking_speed[:-1], 0.0) * tracer[:-1]
        + jnp.minimum(sinking_speed[:-1], 0.0) * tracer[1:]
    )
    flux_lon = jnp.maximum(east_rate, 0.0) * tracer + jnp.minimum(east_rate, 0.0) * jnp.roll(
        tracer, -1, axis=3
    )
    div_lat = (flux_lat[:, :, 1:] - flux_lat[:, :, :-1])[1:-1]
    vertical_divergence = (flux_lev[1:] - flux_lev[:-1])[:, :, 1:-1]
    div_lon = (flux_lon - jnp.roll(flux_lon, 1, axis=3))[1:-1, :, 1:-1]
    return tracer[1:-1, :, 1:-1] - div_lat - vertical_divergence - div_lon


def radiate(inputs, w_rad_in, radiative_final_weights):
    levels, nfield = (inputs.shape[0], inputs.shape[1])
    rad_hidden = jax.nn.gelu(
        lax.dot_general(
            inputs,
            w_rad_in.reshape(levels, nfield, -1),
            (((0, 1), (0, 1)), ((), ())),
            preferred_element_type=jnp.float32,
        )
    ).astype(jnp.bfloat16)
    return lax.dot_general(
        radiative_final_weights,
        rad_hidden,
        (((0,), (1,)), ((), ())),
        preferred_element_type=jnp.float32,
    )


def physics(remapped, w_in, w_out):
    levels, tracer_fields = (remapped.shape[0], remapped.shape[1])
    inputs_bf = remapped.astype(jnp.bfloat16)
    hidden = jax.nn.gelu(
        lax.dot_general(
            inputs_bf,
            w_in.reshape(levels, tracer_fields, -1),
            (((0, 1), (0, 1)), ((), ())),
            preferred_element_type=jnp.float32,
        )
    ).astype(jnp.bfloat16)
    tendency = lax.dot_general(
        w_out.reshape(-1, levels, tracer_fields),
        hidden,
        (((0,), (1,)), ((), ())),
        preferred_element_type=jnp.float32,
    )
    return remapped + tendency


def on_device(
    state,
    cour_lat,
    cour_lev,
    cour_lon,
    remap_weight,
    w_in,
    w_out,
    w_rad_in,
    radiative_final_weights,
    day_list,
    day_count,
):
    lev_dev, tracer_fields, lat_dev, lon_cells = state.shape
    split_count = lax.axis_size("lev")
    all_rows = lat_dev * lax.axis_size("lat")
    every_level_grid = lev_dev * split_count
    row_ids = lax.axis_index("lat") * lat_dev + jnp.arange(lat_dev)
    level_ids = lax.axis_index("lev") * lev_dev + jnp.arange(lev_dev)
    masked_lat = cour_lat * (row_ids < all_rows - 1).astype(jnp.float32)[None, :, None]
    masked_lev = cour_lev * (level_ids < every_level_grid - 1).astype(jnp.float32)[:, None, None]
    courants = jnp.stack([masked_lat, masked_lev, cour_lon], axis=1)
    tracer = state
    padded = with_halo(jnp.concatenate([tracer, courants], axis=1), (("lat", 2), ("lev", 0)), 1)
    tracer = advance(
        padded[:, :tracer_fields],
        padded[:, tracer_fields : tracer_fields + 1],
        padded[:, tracer_fields + 1 : tracer_fields + 2],
        padded[:, tracer_fields + 2 : tracer_fields + 3],
    )
    columns_per_part = lat_dev * lon_cells // split_count
    blocks = tracer.reshape(lev_dev, tracer_fields, split_count, columns_per_part)
    matrix = jnp.eye(every_level_grid, dtype=jnp.float32) + remap_weight
    values = lax.all_to_all(blocks, "lev", split_axis=2, concat_axis=0, tiled=True)
    remapped = jnp.dot(
        matrix, values.reshape(values.shape[0], -1), precision=lax.Precision.HIGHEST
    ).reshape(values.shape)
    remapped = remapped.reshape(every_level_grid, tracer_fields, columns_per_part)
    parameterized_forcing = physics(remapped, w_in, w_out)
    rad_in = parameterized_forcing[:, :RADF].astype(jnp.bfloat16)
    day_order = day_list.reshape(-1)
    day_total = day_count.reshape(())
    ranks = jnp.arange(columns_per_part, dtype=jnp.int32)
    profile_enabled_flag = (
        jnp.zeros((columns_per_part,), jnp.bool_).at[day_order].set(ranks < day_total * DB)
    )
    warming_tendency = radiate(rad_in, w_rad_in, radiative_final_weights)
    atmosphere_warmth = parameterized_forcing[:, 0] + jnp.where(
        profile_enabled_flag[None, :], warming_tendency, 0.0
    )
    step_result = (
        parameterized_forcing.at[:, 0]
        .set(atmosphere_warmth)
        .reshape(every_level_grid, tracer_fields, 1, columns_per_part)
    )
    returned_cols = lax.all_to_all(step_result, "lev", split_axis=0, concat_axis=2, tiled=True)
    return returned_cols.reshape(lev_dev, tracer_fields, lat_dev, lon_cells)


def solution(mesh):
    placed = (
        P("lev", None, "lat", None),
        P("lev", "lat", None),
        P("lev", "lat", None),
        P("lev", "lat", None),
        P(),
        P(),
        P(),
        P(),
        P(),
        P("lat", "lev", None),
        P("lat", "lev"),
    )
    return jax.shard_map(
        on_device,
        mesh=mesh,
        in_specs=placed,
        out_specs=P("lev", None, "lat", None),
        check_vma=False,
    )
```

profile of v0, /device:TPU:12, one launch (start us, length us, event | category | flops | bytes accessed | tf_op | source)
XLA Modules:
  0.0 154.0 jit_solution(16474547105826804110)
XLA Ops:
  0.0 2.0 %copy.84 = f32[8,16,8,256]{3,0,2,1:T(8,128)S(1)} copy(f32[8,16,8,256]{3,2,1,0:T(8,128)} %param.13) | data formatting | bytes 2097152 | tf_op args[0]
  2.0 0.9 fusion.79
  2.9 0.9 copy_bitcast_fusion
  3.9 2.8 %collective-permute-start.1 = (f32[8,19,1,256]{3,0,2,1:T(8,128)S(1)}, f32[8,19,1,256]{3,0,2,1:T(8,128)S(1)}, u32[]{:S(2)}, u32[]{:S(2)}) collective-permute-start(f32[8,19,1,256]{3,0,2,1:T(8,128)S(1)} %get-tuple-element.30), channel_id=1, source_target_pairs={{16,0},{32,16},{48,32},{64,48},{80,64},{96,80},{112,96},{128,112},... | collective-permute-start | bytes 466952 | tf_op jit(solution)/shard_map/ppermute | solution.py:20
  6.7 1.9 %collective-permute-start = (f32[8,19,1,256]{3,0,2,1:T(8,128)S(1)}, f32[8,19,1,256]{3,0,2,1:T(8,128)S(1)}, u32[]{:S(2)}, u32[]{:S(2)}) collective-permute-start(f32[8,19,1,256]{3,0,2,1:T(8,128)S(1)} %get-tuple-element.29), channel_id=1, source_target_pairs={{0,16},{16,32},{32,48},{48,64},{64,80},{80,96},{96,112},{112,128},... | collective-permute-start | bytes 466952 | tf_op jit(solution)/shard_map/ppermute | solution.py:18
  9.5 3.7 %collective-permute-done = f32[8,19,1,256]{3,0,2,1:T(8,128)S(1)} collective-permute-done((f32[8,19,1,256]{3,0,2,1:T(8,128)S(1)}, f32[8,19,1,256]{3,0,2,1:T(8,128)S(1)}, u32[]{:S(2)}, u32[]{:S(2)}) %collective-permute-start) | collective-permute-done | bytes 155680 | tf_op jit(solution)/shard_map/ppermute | solution.py:18
  13.5 7.0 %collective-permute-start.3 = (f32[1,19,10,256]{3,1,2,0:T(8,128)S(1)}, f32[1,19,10,256]{3,1,2,0:T(8,128)S(1)}, u32[]{:S(2)}, u32[]{:S(2)}) collective-permute-start(f32[1,19,10,256]{3,1,2,0:T(8,128)S(1)} %copy.81), channel_id=1, source_target_pairs={{1,0},{2,1},{3,2},{4,3},{5,4},{6,5},{7,6},{8,7},{9,8},{10,9},{11,1... | collective-permute-start | bytes 583688 | tf_op jit(solution)/shard_map/ppermute | solution.py:20
  20.6 1.9 %collective-permute-start.2 = (f32[1,19,10,256]{3,1,2,0:T(8,128)S(1)}, f32[1,19,10,256]{3,1,2,0:T(8,128)S(1)}, u32[]{:S(2)}, u32[]{:S(2)}) collective-permute-start(f32[1,19,10,256]{3,1,2,0:T(8,128)S(1)} %copy.80), channel_id=1, source_target_pairs={{0,1},{1,2},{2,3},{3,4},{4,5},{5,6},{6,7},{7,8},{8,9},{9,10},{10,1... | collective-permute-start | bytes 583688 | tf_op jit(solution)/shard_map/ppermute | solution.py:18
  22.5 6.4 %collective-permute-done.3 = f32[1,19,10,256]{3,1,2,0:T(8,128)S(1)} collective-permute-done((f32[1,19,10,256]{3,1,2,0:T(8,128)S(1)}, f32[1,19,10,256]{3,1,2,0:T(8,128)S(1)}, u32[]{:S(2)}, u32[]{:S(2)}) %collective-permute-start.3) | collective-permute-done | bytes 194592 | tf_op jit(solution)/shard_map/ppermute | solution.py:20
  29.1 10.2 %collective-permute-done.2 = f32[1,19,10,256]{3,1,2,0:T(8,128)S(1)} collective-permute-done((f32[1,19,10,256]{3,1,2,0:T(8,128)S(1)}, f32[1,19,10,256]{3,1,2,0:T(8,128)S(1)}, u32[]{:S(2)}, u32[]{:S(2)}) %collective-permute-start.2) | collective-permute-done | bytes 194592 | tf_op jit(solution)/shard_map/ppermute | solution.py:18
  39.6 1.0 pad_maximum_fusion
  41.5 0.9 fusion.4
  42.9 0.9 fusion.6
  45.7 1.4 fusion.22
  47.1 1.3 copy.87
  48.4 2.3 %reshape.107 = f32[8,16,16,128]{3,2,1,0:T(8,128)} reshape(f32[8,16,8,256]{3,2,1,0:T(8,128)} %copy.87) | data formatting | bytes 2097152 | tf_op jit(solution)/shard_map/reshape | solution.py:114
  50.7 2.5 %copy.88 = f32[8,16,16,128]{3,1,0,2:T(8,128)} copy(f32[8,16,16,128]{3,2,1,0:T(8,128)} %reshape.107) | data formatting | bytes 2097152 | tf_op jit(solution)/shard_map/reshape | solution.py:114
  53.2 7.2 %all-to-all-start = ((f32[8,16,16,128]{3,1,0,2:T(8,128)}), f32[8,16,16,128]{3,1,0,2:T(8,128)}, u32[]{:S(2)}, u32[]{:S(2)}) async-start(f32[8,16,16,128]{3,1,0,2:T(8,128)} %copy.88), calls=%async_computation | async-start | bytes 2097152 | tf_op jit(solution)/shard_map/all_to_all | solution.py:116
  60.4 4.7 %copy.92 = bf16[768,2048]{0,1:T(8,128)(2,1)} copy(bf16[768,2048]{1,0:T(8,128)(2,1)} %param.19) | data formatting | bytes 6291456 | tf_op args[6]
  65.1 2.3 %reshape.113 = bf16[128,4,1024]{2,1,0:T(4,128)(2,1)} reshape(bf16[512,1024]{1,0:T(8,128)(2,1)} %param.20) | data formatting | bytes 2097152 | tf_op jit(solution)/shard_map/reshape | solution.py:50
  68.1 1.2 scatter_custom_fusion
  69.3 18.5 %all-to-all-done = f32[8,16,16,128]{3,1,0,2:T(8,128)} async-done(((f32[8,16,16,128]{3,1,0,2:T(8,128)}), f32[8,16,16,128]{3,1,0,2:T(8,128)}, u32[]{:S(2)}, u32[]{:S(2)}) %all-to-all-start) | async-done | bytes 1048608 | tf_op jit(solution)/shard_map/all_to_all | solution.py:116
  87.8 2.5 %copy.141 = f32[16,8,16,128]{3,1,2,0:T(8,128)} copy(f32[16,8,16,128]{3,2,1,0:T(8,128)} %bitcast.36) | data formatting | bytes 2097152
  90.3 2.5 %copy.89 = f32[2048,128]{1,0:T(8,128)} copy(f32[2048,128]{0,1:T(8,128)} %bitcast.100) | data formatting | bytes 2097152 | tf_op jit(solution)/shard_map/dot_general | solution.py:117
  92.9 3.2 %fusion.76 = f32[128,16,128]{2,0,1:T(8,128)} fusion(f32[16,128,128]{2,1,0:T(8,128)} %bitcast.101, f32[128,128]{1,0:T(8,128)S(1)} %copy-done.2), kind=kOutput, calls=%fused_computation.92 | convolution fusion | flops 402702336 | bytes 2162688 | tf_op jit(solution)/shard_map/dot_general | solution.py:117
  96.1 7.3 %fusion.12 = f32[128,16,128]{2,0,1:T(8,128)} fusion(f32[128,16,128]{2,0,1:T(8,128)} %fusion.76, bf16[768,128,16]{0,2,1:T(8,128)(2,1)} %bitcast.103, bf16[128,16,768]{2,1,0:T(8,128)(2,1)S(1)} %bitcast.98), kind=kOutput, calls=%fused_computation.28 | convolution fusion | flops 806715392 | bytes 8388608 | tf_op jit(solution)/shard_map/dot_general | solution.py:74
  103.4 2.3 %copy.142 = f32[128,16,1,128]{3,0,1,2:T(8,128)} copy(f32[128,16,1,128]{3,0,1,2:T(8,128)} %bitcast.104) | data formatting | bytes 2097152
  105.7 2.7 %fusion.21 = f32[128,16,1,128]{3,0,1,2:T(8,128)} fusion(f32[128,16,1,128]{3,0,1,2:T(8,128)} %copy.142, bf16[1024,128]{1,0:T(8,128)(2,1)S(1)} %copy-done.3, bf16[128,4,1024]{2,1,0:T(4,128)(2,1)} %reshape.113, f32[128,16,128]{2,0,1:T(8,128)} %fusion.12, pred[128]{0:T(512)(128)(4,1)S(1)} %scatter_custom_fusion), kind=kOutput, calls=%fused_computation.35 | convolution fusion | flops 169246720 | bytes 2490496 | tf_op jit(solution)/shard_map/dot_general | solution.py:55
  108.5 1.8 %copy.99 = f32[128,16,1,128]{3,1,2,0:T(8,128)S(1)} copy(f32[128,16,1,128]{3,0,1,2:T(8,128)} %fusion.21) | data formatting | bytes 2097152 | tf_op jit(solution)/shard_map/scatter | solution.py:135
  110.3 39.6 %all_to_all.30 = f32[128,16,1,128]{3,1,2,0:T(8,128)S(1)} all-to-all(f32[128,16,1,128]{3,1,2,0:T(8,128)S(1)} %copy.99), channel_id=1, replica_groups=mesh['lat'=64,'lev'=16] {'lev'}, dimensions={0} | all-to-all | bytes 2097152 | tf_op jit(solution)/shard_map/all_to_all | solution.py:138
  149.9 1.6 %copy.100 = f32[8,16,16,1,128]{4,2,1,0,3:T(8,128)} copy(f32[8,16,16,1,128]{4,1,0,2,3:T(8,128)S(1)} %bitcast.102) | data formatting | bytes 2097152 | tf_op jit(solution)/shard_map/all_to_all | solution.py:138
  151.5 2.5 %reshape.115 = f32[8,16,8,256]{3,2,1,0:T(8,128)} reshape(f32[8,16,16,1,128]{4,2,1,0,3:T(8,128)} %copy.100) | data formatting | bytes 2097152 | tf_op jit(solution)/shard_map/reshape | solution.py:139
  (31 shorter events, 4.9 us)
Async XLA Ops:
  0.0 96.1 %copy-start = (bf16[2048,768]{1,0:T(8,128)(2,1)S(1)}, bf16[2048,768]{1,0:T(8,128)(2,1)}, u32[]{:S(2)}) copy-start(bf16[2048,768]{1,0:T(8,128)(2,1)} %param.18) | copy-start | bytes 9437188
  3.9 5.6 %collective-permute-start.1 = (f32[8,19,1,256]{3,0,2,1:T(8,128)S(1)}, f32[8,19,1,256]{3,0,2,1:T(8,128)S(1)}, u32[]{:S(2)}, u32[]{:S(2)}) collective-permute-start(f32[8,19,1,256]{3,0,2,1:T(8,128)S(1)} %get-tuple-element.30), channel_id=1, source_target_pairs={{16,0},{32,16},{48,32},{64,48},{80,64},{96,80},{112,96},{128,112},... | collective-permute-start | bytes 466952 | tf_op jit(solution)/shard_map/ppermute | solution.py:20
  6.7 6.5 %collective-permute-start = (f32[8,19,1,256]{3,0,2,1:T(8,128)S(1)}, f32[8,19,1,256]{3,0,2,1:T(8,128)S(1)}, u32[]{:S(2)}, u32[]{:S(2)}) collective-permute-start(f32[8,19,1,256]{3,0,2,1:T(8,128)S(1)} %get-tuple-element.29), channel_id=1, source_target_pairs={{0,16},{16,32},{32,48},{48,64},{64,80},{80,96},{96,112},{112,128},... | collective-permute-start | bytes 466952 | tf_op jit(solution)/shard_map/ppermute | solution.py:18
  13.5 15.4 %collective-permute-start.3 = (f32[1,19,10,256]{3,1,2,0:T(8,128)S(1)}, f32[1,19,10,256]{3,1,2,0:T(8,128)S(1)}, u32[]{:S(2)}, u32[]{:S(2)}) collective-permute-start(f32[1,19,10,256]{3,1,2,0:T(8,128)S(1)} %copy.81), channel_id=1, source_target_pairs={{1,0},{2,1},{3,2},{4,3},{5,4},{6,5},{7,6},{8,7},{9,8},{10,9},{11,1... | collective-permute-start | bytes 583688 | tf_op jit(solution)/shard_map/ppermute | solution.py:20
  20.6 18.8 %collective-permute-start.2 = (f32[1,19,10,256]{3,1,2,0:T(8,128)S(1)}, f32[1,19,10,256]{3,1,2,0:T(8,128)S(1)}, u32[]{:S(2)}, u32[]{:S(2)}) collective-permute-start(f32[1,19,10,256]{3,1,2,0:T(8,128)S(1)} %copy.80), channel_id=1, source_target_pairs={{0,1},{1,2},{2,3},{3,4},{4,5},{5,6},{6,7},{7,8},{8,9},{9,10},{10,1... | collective-permute-start | bytes 583688 | tf_op jit(solution)/shard_map/ppermute | solution.py:18
  44.5 1.2 copy-start.1
  53.2 34.6 %all-to-all-start = ((f32[8,16,16,128]{3,1,0,2:T(8,128)}), f32[8,16,16,128]{3,1,0,2:T(8,128)}, u32[]{:S(2)}, u32[]{:S(2)}) async-start(f32[8,16,16,128]{3,1,0,2:T(8,128)} %copy.88), calls=%async_computation | async-start | bytes 2097152 | tf_op jit(solution)/shard_map/all_to_all | solution.py:116
  60.4 7.6 %copy-start.4 = (s32[1,1,128]{2,1,0:T(1,128)S(1)}, s32[1,1,128]{2,1,0:T(1,128)}, u32[]{:S(2)}) copy-start(s32[1,1,128]{2,1,0:T(1,128)} %param.22) | copy-start | bytes 1540
  67.4 25.5 %copy-start.2 = (f32[128,128]{1,0:T(8,128)S(1)}, f32[128,128]{1,0:T(8,128)}, u32[]{:S(2)}) copy-start(f32[128,128]{1,0:T(8,128)} %param.17) | copy-start | bytes 196612
  96.1 9.6 %copy-start.3 = (bf16[1024,128]{1,0:T(8,128)(2,1)S(1)}, bf16[1024,128]{1,0:T(8,128)(2,1)}, u32[]{:S(2)}) copy-start(bf16[1024,128]{1,0:T(8,128)(2,1)} %param.21) | copy-start | bytes 786436
where the time goes:
time: 155 us; the launch traced here: 154 us
  waiting for transfers between devices  39.8 us (26%)
  blocking collectives  39.6 us (26%)
  local copies, waits for them, and re-layouts  32.7 us (21%)
  starting transfers between devices  20.8 us (13%)
  matrix products  13.3 us (9%)
  other arithmetic  6.79 us (4%)
    all_to_all x1, blocking collectives, on_device(): lax.all_to_all(step_result, 'lev', split_axis=0, concat_axis=2, tiled=True)  39.6 us
    all_to_all x1, waiting for transfers between devices, on_device(): lax.all_to_all(blocks, 'lev', split_axis=2, concat_axis=0, tiled=True)  18.5 us
    ppermute x2, waiting for transfers between devices, with_halo(): lax.ppermute(tail, axis, [(i, (i + 1) % count) for i in range(ends)])  14 us
    unnamed x14, local copies, waits for them, and re-layouts  12.1 us
    ppermute x2, starting transfers between devices, with_halo(): lax.ppermute(head, axis, [((i + 1) % count, i) for i in range(ends)])  9.78 us
    ppermute x2, waiting for transfers between devices, with_halo(): lax.ppermute(head, axis, [((i + 1) % count, i) for i in range(ends)])  7.35 us
    dot_general x1, matrix products, physics(): lax.dot_general(w_out.reshape(-1, levels, tracer_fields), hidden, (((0,),...  7.33 us
    all_to_all x1, starting transfers between devices, on_device(): lax.all_to_all(blocks, 'lev', split_axis=2, concat_axis=0, tiled=True)  7.22 us
  transfers between devices with their start and end apart: 5, of which 5 were waited for; matrix products, arithmetic and copies ran while one was open for 5% of the time, Pallas kernels for 0%

commit v1 on v0

v1 whole, which is shorter than its diff:
```python
import functools

import jax
import jax.numpy as jnp
from jax import lax
from jax.experimental import pallas as pl
from jax.experimental.pallas import tpu as pltpu
from jax.sharding import PartitionSpec as P

RADF = 4
DB = 16
LANES = 128
BF = jnp.bfloat16
F32 = jnp.float32
VMEM_LIMIT = 24 * 1024 * 1024
SPREAD = 7.0


def call(kernel, name, out_shape, in_specs, scratch=(), flops=0, moved=0, limit=VMEM_LIMIT):
    vmem = pl.BlockSpec(memory_space=pltpu.VMEM)
    return pl.pallas_call(
        kernel,
        name=name,
        out_shape=out_shape,
        in_specs=in_specs,
        out_specs=jax.tree.map(lambda _: vmem, out_shape),
        scratch_shapes=list(scratch),
        compiler_params=pltpu.CompilerParams(vmem_limit_bytes=limit),
        cost_estimate=pl.CostEstimate(flops=flops, bytes_accessed=moved, transcendentals=0),
    )


def pack_kernel(state, cour_lat, cour_lev, lat_up, lat_dn, lev_up, lev_dn):
    nlev, nf, nrow, _ = state.shape
    for level in range(nlev):
        for half in range(nf // 8):
            rows = slice(level * nf + half * 8, level * nf + half * 8 + 8)
            block = state[level, half * 8 : half * 8 + 8]
            lat_up[rows, :] = block[:, nrow - 1, :].astype(BF)
            lat_dn[rows, :] = block[:, 0, :].astype(BF)
    lat_up[nlev * nf :, :] = cour_lat[:, nrow - 1, :].astype(BF)
    for field in range(nf):
        rows = slice(field * nrow, field * nrow + nrow)
        lev_up[rows, :] = state[nlev - 1, field].astype(BF)
        lev_dn[rows, :] = state[0, field].astype(BF)
    lev_up[nf * nrow :, :] = cour_lev[nlev - 1].astype(BF)


def transport_kernel(
    ends, state, cour_lat, cour_lev, cour_lon, from_south, from_north, from_above, from_below,
    moved, sent, south, north, above, below, turned,
):
    nlev, nf, nrow, nlon = state.shape
    south[...] = from_south[...].astype(F32)
    north[...] = from_north[...].astype(F32)
    above[...] = from_above[...].astype(F32)
    below[...] = from_below[...].astype(F32)
    row = lax.broadcasted_iota(jnp.int32, (nrow, nlon), 0)
    first_row, last_row = row == 0, row == nrow - 1
    wide = (nrow, nlon)
    closed_lat = jnp.logical_and(last_row, ends[0] == 1)
    open_lev = jnp.where(ends[1] == 1, 0.0, 1.0).astype(F32)

    def lev_rate(level):
        if level < 0:
            return above[nf * nrow : nf * nrow + nrow, :]
        rate = cour_lev[level]
        return rate * open_lev if level == nlev - 1 else rate

    for level in range(nlev):
        n = jnp.where(closed_lat, 0.0, cour_lat[level])
        halo = jnp.broadcast_to(south[nlev * nf + level : nlev * nf + level + 1, :], wide)
        ns = jnp.where(first_row, halo, pltpu.roll(n, 1, 0))
        d, du = lev_rate(level), lev_rate(level - 1)
        e = cour_lon[level]
        ew = pltpu.roll(e, 1, 1)
        mid = (
            1.0
            - (jnp.maximum(n, 0.0) - jnp.minimum(ns, 0.0))
            - (jnp.maximum(d, 0.0) - jnp.minimum(du, 0.0))
            - (jnp.maximum(e, 0.0) - jnp.minimum(ew, 0.0))
        )
        c_n, c_s = jnp.minimum(n, 0.0), jnp.maximum(ns, 0.0)
        c_d, c_u = jnp.minimum(d, 0.0), jnp.maximum(du, 0.0)
        c_e, c_w = jnp.minimum(e, 0.0), jnp.maximum(ew, 0.0)
        for field in range(nf):
            q = state[level, field]
            at = level * nf + field
            rows = slice(field * nrow, field * nrow + nrow)
            qs = jnp.where(
                first_row, jnp.broadcast_to(south[at : at + 1, :], wide), pltpu.roll(q, 1, 0)
            )
            qn = jnp.where(
                last_row, jnp.broadcast_to(north[at : at + 1, :], wide), pltpu.roll(q, nrow - 1, 0)
            )
            qu = above[rows, :] if level == 0 else state[level - 1, field]
            qd = below[rows, :] if level == nlev - 1 else state[level + 1, field]
            qe = pltpu.roll(q, nlon - 1, 1)
            qw = pltpu.roll(q, 1, 1)
            t = (
                (mid * q + (c_s * qs - c_n * qn))
                + (c_u * qu - c_d * qd)
                + (c_w * qw - c_e * qe)
            )
            moved[level, field] = t
            for half in range(nlon // LANES):
                turned[pl.ds(((field * 2 + half) * nlev + level) * nrow, nrow), :] = t[
                    :, half * LANES : half * LANES + LANES
                ]
    for field in range(nf):
        for half in range(nlon // LANES):
            for r in range(nrow):
                first = (field * 2 + half) * nlev * nrow + r
                tile = turned[pl.ds(first, nlev, stride=nrow), :]
                sent[r * 2 + half, field] = jnp.exp2(tile * SPREAD).astype(BF)


def gelu(x):
    return 0.5 * x * (1.0 + jnp.tanh(0.7978845608028654 * (x + 0.044715 * (x * x * x))))


def column_kernel(
    count, got, remap, w_in, w_out, w_rad, w_heat, day, back,
    whole, split, remapped, extra, hidden, rad_in, rad_hidden, heat,
):
    ngroup, nf, nlev, ncol = got.shape
    levels = ngroup * nlev
    pair = 2 * levels
    w = remap[...]
    high = w.astype(BF)
    low = (w - high.astype(F32)).astype(BF)
    both = jnp.concatenate([high, low], axis=1)
    for field in range(nf):
        code = got[:, field].astype(F32).reshape(levels, ncol)
        t = jnp.log2(code) * (1.0 / SPREAD)
        lanes = slice(field * ncol, field * ncol + ncol)
        th = t.astype(BF)
        whole[:, lanes] = t
        split[:levels, lanes] = th
        split[levels:pair, lanes] = th
        split[pair:, lanes] = (t - th.astype(F32)).astype(BF)
    for two in range(nf // 2):
        lanes = slice(two * 2 * ncol, two * 2 * ncol + 2 * ncol)
        wt = jnp.dot(both, split[:pair, lanes], preferred_element_type=F32) + jnp.dot(
            high, split[pair:, lanes], preferred_element_type=F32
        )
        x = (whole[:, lanes] + wt).astype(BF)
        for k in range(2):
            rows = slice((two * 2 + k) * levels, (two * 2 + k + 1) * levels)
            extra[rows, :] = wt[:, k * ncol : k * ncol + ncol]
            remapped[rows, :] = x[:, k * ncol : k * ncol + ncol]

    nhid = w_in.shape[0]
    chunk = 256

    @pl.loop(0, nhid // chunk)
    def _(i):
        rows = pl.ds(pl.multiple_of(i * chunk, chunk), chunk)
        hidden[rows, :] = gelu(
            jnp.dot(w_in[rows, :], remapped[...], preferred_element_type=F32)
        ).astype(BF)

    @pl.loop(0, nf * levels // pair)
    def _(i):
        rows = pl.ds(pl.multiple_of(i * pair, pair), pair)
        extra[rows, :] = extra[rows, :] + jnp.dot(
            w_out[rows, :], hidden[...], preferred_element_type=F32
        )

    for field in range(RADF):
        rows = slice(field * levels, field * levels + levels)
        lanes = slice(field * ncol, field * ncol + ncol)
        rad_in[rows, :] = (whole[:, lanes] + extra[rows, :]).astype(BF)

    @pl.loop(0, w_rad.shape[0] // chunk)
    def _(i):
        rows = pl.ds(pl.multiple_of(i * chunk, chunk), chunk)
        rad_hidden[rows, :] = gelu(
            jnp.dot(w_rad[rows, :], rad_in[...], preferred_element_type=F32)
        ).astype(BF)

    warm = jnp.dot(w_heat[...], rad_hidden[...], preferred_element_type=F32)
    col = lax.broadcasted_iota(jnp.int32, (ncol, ncol), 0)
    rank = lax.broadcasted_iota(jnp.int32, (ncol, ncol), 1)
    hit = jnp.logical_and(day[...] == col, rank < count[0] * DB)
    lit = lax.dot_general(
        jnp.ones((8, ncol), BF),
        jnp.where(hit, 1.0, 0.0).astype(BF),
        (((1,), (1,)), ((), ())),
        preferred_element_type=F32,
    )
    heat[...] = jnp.where(jnp.broadcast_to(lit[:1, :], warm.shape) > 0.5, warm, 0.0)
    extra[:levels, :] = extra[:levels, :] + heat[...]

    for field in range(nf):
        rows = slice(field * levels, field * levels + levels)
        back[:, field] = extra[rows, :].reshape(ngroup, nlev, ncol).astype(BF)


def finish_kernel(moved, change, out, turned):
    nlev, nf, nrow, nlon = moved.shape
    for field in range(nf):
        for half in range(nlon // LANES):
            for r in range(nrow):
                turned[pl.ds(((field * 2 + half) * nrow + r) * nlev, nlev), :] = change[
                    r * 2 + half, field
                ].astype(F32)
    for field in range(nf):
        for half in range(nlon // LANES):
            lanes = slice(half * LANES, half * LANES + LANES)
            for level in range(nlev):
                first = (field * 2 + half) * nrow * nlev + level
                out[level, field, :, lanes] = (
                    moved[level, field, :, lanes]
                    + turned[pl.ds(first, nrow, stride=nlev), :]
                )


def on_device(
    state, cour_lat, cour_lev, cour_lon, remap_weight, w_in, w_out, w_rad_in,
    radiative_final_weights, day_list, day_count,
):
    nlev, nf, nrow, nlon = state.shape
    nlat_dev, nlev_dev = lax.axis_size("lat"), lax.axis_size("lev")
    levels = nlev * nlev_dev
    ncol = nrow * nlon // nlev_dev
    vmem = pl.BlockSpec(memory_space=pltpu.VMEM)
    smem = pl.BlockSpec(memory_space=pltpu.SMEM)
    shape = jax.ShapeDtypeStruct

    lat_rows, lev_rows = nlev * nf, nf * nrow
    lat_up, lat_dn, lev_up, lev_dn = call(
        pack_kernel,
        "pack",
        (
            shape((lat_rows + nlev, nlon), BF),
            shape((lat_rows, nlon), BF),
            shape((lev_rows + nrow, nlon), BF),
            shape((lev_rows, nlon), BF),
        ),
        [vmem] * 3,
    )(state, cour_lat, cour_lev)
    up_lat = [(i, i + 1) for i in range(nlat_dev - 1)]
    dn_lat = [(i + 1, i) for i in range(nlat_dev - 1)]
    up_lev = [(i, i + 1) for i in range(nlev_dev - 1)]
    dn_lev = [(i + 1, i) for i in range(nlev_dev - 1)]
    from_above = lax.ppermute(lev_up, "lev", up_lev)
    from_below = lax.ppermute(lev_dn, "lev", dn_lev)
    from_south = lax.ppermute(lat_up, "lat", up_lat)
    from_north = lax.ppermute(lat_dn, "lat", dn_lat)

    ends = jnp.stack(
        [lax.axis_index("lat") == nlat_dev - 1, lax.axis_index("lev") == nlev_dev - 1]
    ).astype(jnp.int32)
    groups = 2 * nrow
    moved, sent = call(
        transport_kernel,
        "transport",
        (shape(state.shape, F32), shape((groups, nf, nlev, LANES), BF)),
        [smem] + [vmem] * 8,
        [
            pltpu.VMEM((lat_rows + nlev, nlon), F32),
            pltpu.VMEM((lat_rows, nlon), F32),
            pltpu.VMEM((lev_rows + nrow, nlon), F32),
            pltpu.VMEM((lev_rows, nlon), F32),
            pltpu.VMEM((nf * 2 * nlev * nrow, LANES), F32),
        ],
    )(ends, state, cour_lat, cour_lev, cour_lon, from_south, from_north, from_above, from_below)

    got = lax.all_to_all(sent, "lev", split_axis=0, concat_axis=0, tiled=True)

    nhid, nrad = w_in.shape[1], w_rad_in.shape[1]
    w_in_t = w_in.reshape(levels, nf, nhid).transpose(2, 1, 0).reshape(nhid, nf * levels)
    w_out_t = w_out.reshape(nhid, levels, nf).transpose(2, 1, 0).reshape(nf * levels, nhid)
    w_rad_t = w_rad_in.reshape(levels, RADF, nrad).transpose(2, 1, 0).reshape(nrad, RADF * levels)
    w_heat_t = radiative_final_weights.T
    back = call(
        column_kernel,
        "columns",
        shape(got.shape, BF),
        [smem] + [vmem] * 7,
        [
            pltpu.VMEM((levels, nf * ncol), F32),
            pltpu.VMEM((3 * levels, nf * ncol), BF),
            pltpu.VMEM((nf * levels, ncol), BF),
            pltpu.VMEM((nf * levels, ncol), F32),
            pltpu.VMEM((nhid, ncol), BF),
            pltpu.VMEM((RADF * levels, ncol), BF),
            pltpu.VMEM((nrad, ncol), BF),
            pltpu.VMEM((levels, ncol), F32),
        ],
    )(
        day_count.reshape(1), got, remap_weight, w_in_t, w_out_t, w_rad_t, w_heat_t,
        day_list.reshape(1, -1),
    )

    change = lax.all_to_all(back, "lev", split_axis=0, concat_axis=0, tiled=True)
    return call(
        finish_kernel,
        "finish",
        shape(state.shape, F32),
        [vmem] * 2,
        [pltpu.VMEM((nf * 2 * nlev * nrow, LANES), F32)],
    )(moved, change)


def solution(mesh):
    placed = (
        P("lev", None, "lat", None),
        P("lev", "lat", None),
        P("lev", "lat", None),
        P("lev", "lat", None),
        P(),
        P(),
        P(),
        P(),
        P(),
        P("lat", "lev", None),
        P("lat", "lev"),
    )
    return jax.shard_map(
        on_device,
        mesh=mesh,
        in_specs=placed,
        out_specs=P("lev", None, "lat", None),
        check_vma=False,
    )
```

time: 155 us -> 109 us (0.70)
  the two profiles are of different devices: /device:TPU:12 before, /device:TPU:512 now
where the time goes in v1:
time: 109 us; the launch traced here: 108 us
  local copies, waits for them, and re-layouts  37.8 us (35%)
  starting transfers between devices  28 us (26%)
  blocking collectives  25.9 us (24%)
  Pallas kernels  10.3 us (9%)
  waiting for transfers between devices  4.78 us (4%)
    all_to_all x1, blocking collectives, on_device(): lax.all_to_all(back, 'lev', split_axis=0, concat_axis=0, tiled=True)  25.9 us
    unnamed x30, local copies, waits for them, and re-layouts  22.1 us
    all_to_all x1, starting transfers between devices, on_device(): got = lax.all_to_all(sent, 'lev', split_axis=0, concat_axis=0, tiled=True)  13.9 us
    ppermute x1, starting transfers between devices, on_device(): from_north = lax.ppermute(lat_dn, 'lat', dn_lat)  7.27 us
    pallas_call x1, Pallas kernels, on_device(): call(column_kernel, 'columns', shape(got.shape, BF), [smem] + [vmem] * 7,...  6.42 us
    reshape x2, local copies, waits for them, and re-layouts, on_device(): w_rad_in.reshape(levels, RADF, nrad).transpose(2, 1, 0)  5.75 us
    reshape x1, local copies, waits for them, and re-layouts, on_device(): w_in.reshape(levels, nf, nhid).transpose(2, 1, 0).reshape(nhid, nf * levels)  5.4 us
    transpose x1, local copies, waits for them, and re-layouts, on_device(): w_out.reshape(nhid, levels, nf).transpose(2, 1, 0)  4.55 us
  transfers between devices with their start and end apart: 5, of which 2 were waited for; matrix products, arithmetic and copies ran while one was open for 25% of the time, Pallas kernels for 0%

profile of v1, /device:TPU:512, one launch (start us, length us, event | category | flops | bytes accessed | tf_op | source)
XLA Modules:
  0.0 107.6 jit_solution(13344334362848396252)
XLA Ops:
  0.0 1.2 %copy-done.2 = f32[8,16,8,256]{3,2,1,0:T(8,128)S(1)} copy-done((f32[8,16,8,256]{3,2,1,0:T(8,128)S(1)}, f32[8,16,8,256]{3,2,1,0:T(8,128)}, u32[]{:S(2)}) %copy-start.2) | copy-done | bytes 1048600
  1.2 0.8 copy-done.6
  2.1 0.8 copy-done.8
  2.9 0.2 pack.1
  3.1 1.9 %collective-permute-start = (bf16[136,256]{1,0:T(8,128)(2,1)S(1)}, bf16[136,256]{1,0:T(8,128)(2,1)S(1)}, u32[]{:S(2)}, u32[]{:S(2)}) collective-permute-start(bf16[136,256]{1,0:T(8,128)(2,1)S(1)} %get-tuple-element.11), channel_id=1, source_target_pairs={{0,16},{16,32},{32,48},{48,64},{64,80},{80,96},{96,112},{112,128},... | collective-permute-start | bytes 208904 | tf_op jit(solution)/shard_map/ppermute | solution.py:249
  5.0 3.6 %collective-permute-start.2 = (bf16[136,256]{1,0:T(8,128)(2,1)S(1)}, bf16[136,256]{1,0:T(8,128)(2,1)S(1)}, u32[]{:S(2)}, u32[]{:S(2)}) collective-permute-start(bf16[136,256]{1,0:T(8,128)(2,1)S(1)} %get-tuple-element.13), channel_id=1, source_target_pairs={{0,1},{1,2},{2,3},{3,4},{4,5},{5,6},{6,7},{7,8},{8,9},{9,10},{10,1... | collective-permute-start | bytes 208904 | tf_op jit(solution)/shard_map/ppermute | solution.py:247
  8.7 7.3 %collective-permute-start.1 = (bf16[128,256]{1,0:T(8,128)(2,1)S(1)}, bf16[128,256]{1,0:T(8,128)(2,1)S(1)}, u32[]{:S(2)}, u32[]{:S(2)}) collective-permute-start(bf16[128,256]{1,0:T(8,128)(2,1)S(1)} %get-tuple-element.12), channel_id=1, source_target_pairs={{16,0},{32,16},{48,32},{64,48},{80,64},{96,80},{112,96},{128,112},... | collective-permute-start | bytes 196616 | tf_op jit(solution)/shard_map/ppermute | solution.py:250
  15.9 1.3 %collective-permute-start.3 = (bf16[128,256]{1,0:T(8,128)(2,1)S(1)}, bf16[128,256]{1,0:T(8,128)(2,1)S(1)}, u32[]{:S(2)}, u32[]{:S(2)}) collective-permute-start(bf16[128,256]{1,0:T(8,128)(2,1)S(1)} %get-tuple-element.14), channel_id=1, source_target_pairs={{1,0},{2,1},{3,2},{4,3},{5,4},{6,5},{7,6},{8,7},{9,8},{10,9},{11,1... | collective-permute-start | bytes 196616 | tf_op jit(solution)/shard_map/ppermute | solution.py:248
  17.2 0.1 add_convert_fusion.ends
  17.3 0.5 collective-permute-done.1.from_north
  17.8 4.3 %collective-permute-done.3.from_below = bf16[128,256]{1,0:T(8,128)(2,1)S(1)} collective-permute-done((bf16[128,256]{1,0:T(8,128)(2,1)S(1)}, bf16[128,256]{1,0:T(8,128)(2,1)S(1)}, u32[]{:S(2)}, u32[]{:S(2)}) %collective-permute-start.3) | collective-permute-done | bytes 65568 | tf_op jit(solution)/shard_map/ppermute | solution.py:248
  22.1 0.0 collective-permute-done.from_south
  22.1 1.2 %copy-done.3 = f32[8,16,8,256]{3,2,1,0:T(8,128)S(1)} copy-done((f32[8,16,8,256]{3,2,1,0:T(8,128)S(1)}, f32[8,16,8,256]{3,2,1,0:T(8,128)}, u32[]{:S(2)}) %copy-start.3) | copy-done | bytes 1048600
  23.3 0.8 copy-done.7
  24.2 0.8 copy-done.9
  25.0 0.8 copy-done.11
  25.8 2.4 %transport.1 = (f32[8,16,8,256]{3,2,1,0:T(8,128)S(1)}, bf16[16,16,8,128]{3,2,1,0:T(8,128)(2,1)}) custom-call(s32[2]{0:T(128)S(1)} %add_convert_fusion.ends, f32[8,16,8,256]{3,2,1,0:T(8,128)S(1)} %copy-done.3, f32[8,8,256]{2,1,0:T(8,128)S(1)} %copy-done.7, f32[8,8,256]{2,1,0:T(8,128)S(1)} %copy-done.9, f32[8,8,256]{2,1,0:T(8,128)S(1)} %copy-done.11, ...), custom_call_target="tpu_custom_call" | custom-call | tf_op jit(solution)/shard_map/transport/pallas_call | solution.py:256
  28.2 1.0 copy-done.4
  29.2 13.9 %all-to-all-start = ((bf16[16,16,8,128]{3,2,1,0:T(8,128)(2,1)}), bf16[16,16,8,128]{3,2,1,0:T(8,128)(2,1)}, u32[]{:S(2)}, u32[]{:S(2)}) async-start(bf16[16,16,8,128]{3,2,1,0:T(8,128)(2,1)} %get-tuple-element.16), calls=%async_computation | async-start | bytes 1048576 | tf_op jit(solution)/shard_map/all_to_all | solution.py:270
  43.1 5.4 %copy.16 = bf16[128,16,768]{0,1,2:T(8,128)(2,1)} copy(bf16[128,16,768]{2,1,0:T(8,128)(2,1)} %bitcast.29) | data formatting | bytes 6291456 | tf_op jit(solution)/shard_map/reshape | solution.py:273
  48.5 3.2 %copy.25 = bf16[96,8,16,128]{3,1,2,0:T(8,128)(2,1)S(1)} copy(bf16[96,8,16,128]{3,2,1,0:T(8,128)(2,1)} %bitcast.26) | data formatting | bytes 6291456
  51.7 4.7 %copy.17 = bf16[768,2048]{0,1:T(8,128)(2,1)} copy(bf16[768,2048]{1,0:T(8,128)(2,1)} %param.17) | data formatting | bytes 6291456 | tf_op args[6]
  56.4 4.6 %copy.18 = bf16[16,128,768]{2,1,0:T(8,128)(2,1)} copy(bf16[16,128,768]{2,0,1:T(8,128)(2,1)} %bitcast.27) | data formatting | bytes 6291456 | tf_op jit(solution)/shard_map/transpose | solution.py:274
  61.0 2.3 %reshape.29 = bf16[128,4,1024]{2,1,0:T(4,128)(2,1)} reshape(bf16[512,1024]{1,0:T(8,128)(2,1)} %param.18) | data formatting | bytes 2097152 | tf_op jit(solution)/shard_map/reshape | solution.py:275
  63.2 3.5 %copy.19 = bf16[128,4,1024]{0,1,2:T(4,128)(2,1)} copy(bf16[128,4,1024]{2,1,0:T(4,128)(2,1)} %reshape.29) | data formatting | bytes 2097152 | tf_op jit(solution)/shard_map/reshape | solution.py:275
  66.7 2.4 %copy.26 = bf16[128,8,4,128]{3,1,2,0:T(8,128)(2,1)} copy(bf16[128,8,4,128]{3,2,1,0:T(4,128)(2,1)} %bitcast.28) | data formatting | bytes 2097152
  69.1 1.1 %copy.20 = bf16[1024,128]{0,1:T(8,128)(2,1)S(1)} copy(bf16[1024,128]{1,0:T(8,128)(2,1)} %param.19) | data formatting | bytes 524288 | tf_op args[8]
  70.9 1.9 %copy-done = bf16[16,128,768]{2,1,0:T(8,128)(2,1)S(1)} copy-done((bf16[16,128,768]{2,1,0:T(8,128)(2,1)S(1)}, bf16[16,128,768]{2,1,0:T(8,128)(2,1)}, u32[]{:S(2)}) %copy-start) | copy-done | bytes 3145752
  72.8 1.2 %copy-done.1 = bf16[128,8,4,128]{3,1,2,0:T(8,128)(2,1)S(1)} copy-done((bf16[128,8,4,128]{3,1,2,0:T(8,128)(2,1)S(1)}, bf16[128,8,4,128]{3,1,2,0:T(8,128)(2,1)}, u32[]{:S(2)}) %copy-start.1) | copy-done | bytes 1048600
  74.0 6.4 %columns.1 = bf16[16,16,8,128]{3,2,1,0:T(8,128)(2,1)S(1)} custom-call(s32[1]{0:T(128)} %bitcast.20.count, bf16[16,16,8,128]{3,2,1,0:T(8,128)(2,1)} %all-to-all-done.got, f32[128,128]{1,0:T(8,128)S(1)} %copy-done.10, bf16[768,2048]{1,0:T(8,128)(2,1)S(1)} %bitcast.21, bf16[2048,768]{1,0:T(8,128)(2,1)S(1)} %bitcast.22, bf16[1024,512]{1,0:T(8,128)(2,1)S(1)} %bitcast.23, ...), custom_call_target="tpu_custom_call" | custom-call | tf_op jit(solution)/shard_map/columns/pallas_call | solution.py:277
  80.4 25.9 %all_to_all.10.change = bf16[16,16,8,128]{3,2,1,0:T(8,128)(2,1)S(1)} all-to-all(bf16[16,16,8,128]{3,2,1,0:T(8,128)(2,1)S(1)} %columns.1), channel_id=1, replica_groups=mesh['lat'=64,'lev'=16] {'lev'}, dimensions={0} | all-to-all | bytes 1048576 | tf_op jit(solution)/shard_map/all_to_all | solution.py:297
  106.3 1.2 %finish.1 = f32[8,16,8,256]{3,2,1,0:T(8,128)} custom-call(f32[8,16,8,256]{3,2,1,0:T(8,128)S(1)} %copy-done.5, bf16[16,16,8,128]{3,2,1,0:T(8,128)(2,1)S(1)} %all_to_all.10.change), custom_call_target="tpu_custom_call" | custom-call | tf_op jit(solution)/shard_map/finish/pallas_call | solution.py:298
  (18 shorter events, 0.0 us)
Async XLA Ops:
  0.0 1.2 %copy-start.2 = (f32[8,16,8,256]{3,2,1,0:T(8,128)S(1)}, f32[8,16,8,256]{3,2,1,0:T(8,128)}, u32[]{:S(2)}) copy-start(f32[8,16,8,256]{3,2,1,0:T(8,128)} %state.3) | copy-start | bytes 3145732
  1.2 0.8 copy-start.6
  2.1 0.8 copy-start.8
  3.1 19.0 %collective-permute-start = (bf16[136,256]{1,0:T(8,128)(2,1)S(1)}, bf16[136,256]{1,0:T(8,128)(2,1)S(1)}, u32[]{:S(2)}, u32[]{:S(2)}) collective-permute-start(bf16[136,256]{1,0:T(8,128)(2,1)S(1)} %get-tuple-element.11), channel_id=1, source_target_pairs={{0,16},{16,32},{32,48},{48,64},{64,80},{80,96},{96,112},{112,128},... | collective-permute-start | bytes 208904 | tf_op jit(solution)/shard_map/ppermute | solution.py:249
  5.0 17.0 %collective-permute-start.2 = (bf16[136,256]{1,0:T(8,128)(2,1)S(1)}, bf16[136,256]{1,0:T(8,128)(2,1)S(1)}, u32[]{:S(2)}, u32[]{:S(2)}) collective-permute-start(bf16[136,256]{1,0:T(8,128)(2,1)S(1)} %get-tuple-element.13), channel_id=1, source_target_pairs={{0,1},{1,2},{2,3},{3,4},{4,5},{5,6},{6,7},{7,8},{8,9},{9,10},{10,1... | collective-permute-start | bytes 208904 | tf_op jit(solution)/shard_map/ppermute | solution.py:247
  8.7 9.2 %collective-permute-start.1 = (bf16[128,256]{1,0:T(8,128)(2,1)S(1)}, bf16[128,256]{1,0:T(8,128)(2,1)S(1)}, u32[]{:S(2)}, u32[]{:S(2)}) collective-permute-start(bf16[128,256]{1,0:T(8,128)(2,1)S(1)} %get-tuple-element.12), channel_id=1, source_target_pairs={{16,0},{32,16},{48,32},{64,48},{80,64},{96,80},{112,96},{128,112},... | collective-permute-start | bytes 196616 | tf_op jit(solution)/shard_map/ppermute | solution.py:250
  15.9 6.2 %collective-permute-start.3 = (bf16[128,256]{1,0:T(8,128)(2,1)S(1)}, bf16[128,256]{1,0:T(8,128)(2,1)S(1)}, u32[]{:S(2)}, u32[]{:S(2)}) collective-permute-start(bf16[128,256]{1,0:T(8,128)(2,1)S(1)} %get-tuple-element.14), channel_id=1, source_target_pairs={{1,0},{2,1},{3,2},{4,3},{5,4},{6,5},{7,6},{8,7},{9,8},{10,9},{11,1... | collective-permute-start | bytes 196616 | tf_op jit(solution)/shard_map/ppermute | solution.py:248
  22.1 1.2 %copy-start.3 = (f32[8,16,8,256]{3,2,1,0:T(8,128)S(1)}, f32[8,16,8,256]{3,2,1,0:T(8,128)}, u32[]{:S(2)}) copy-start(f32[8,16,8,256]{3,2,1,0:T(8,128)} %state.3) | copy-start | bytes 3145732
  23.3 0.8 copy-start.7
  24.2 0.8 copy-start.9
  25.0 0.8 copy-start.11
  28.2 1.0 copy-start.4
  29.2 41.6 %all-to-all-start = ((bf16[16,16,8,128]{3,2,1,0:T(8,128)(2,1)}), bf16[16,16,8,128]{3,2,1,0:T(8,128)(2,1)}, u32[]{:S(2)}, u32[]{:S(2)}) async-start(bf16[16,16,8,128]{3,2,1,0:T(8,128)(2,1)} %get-tuple-element.16), calls=%async_computation | async-start | bytes 1048576 | tf_op jit(solution)/shard_map/all_to_all | solution.py:270
  61.0 9.9 %copy-start.10 = (f32[128,128]{1,0:T(8,128)S(1)}, f32[128,128]{1,0:T(8,128)}, u32[]{:S(2)}) copy-start(f32[128,128]{1,0:T(8,128)} %remap.1) | copy-start | bytes 196612
  61.0 9.9 %copy-start.12 = (s32[1,1,128]{2,1,0:T(1,128)S(1)}, s32[1,1,128]{2,1,0:T(1,128)}, u32[]{:S(2)}) copy-start(s32[1,1,128]{2,1,0:T(1,128)} %param.20) | copy-start | bytes 1540
  70.9 1.9 %copy-start = (bf16[16,128,768]{2,1,0:T(8,128)(2,1)S(1)}, bf16[16,128,768]{2,1,0:T(8,128)(2,1)}, u32[]{:S(2)}) copy-start(bf16[16,128,768]{2,1,0:T(8,128)(2,1)} %copy.18) | copy-start | bytes 9437188
  72.8 1.2 %copy-start.1 = (bf16[128,8,4,128]{3,1,2,0:T(8,128)(2,1)S(1)}, bf16[128,8,4,128]{3,1,2,0:T(8,128)(2,1)}, u32[]{:S(2)}) copy-start(bf16[128,8,4,128]{3,1,2,0:T(8,128)(2,1)} %copy.26) | copy-start | bytes 3145732
  74.0 32.3 %copy-start.5 = (f32[8,16,8,256]{3,2,1,0:T(8,128)S(1)}, f32[8,16,8,256]{3,2,1,0:T(8,128)}, u32[]{:S(2)}) copy-start(f32[8,16,8,256]{3,2,1,0:T(8,128)} %copy-done.4) | copy-start | bytes 3145732

commit v2 on v1

v2 whole, which is shorter than its diff:
```python
import jax
import jax.numpy as jnp
from jax import lax
from jax.experimental import pallas as pl
from jax.experimental.pallas import tpu as pltpu
from jax.sharding import PartitionSpec as P

RADF = 4
DB = 16
LANES = 128
BF = jnp.bfloat16
F32 = jnp.float32
VMEM_LIMIT = 16 << 20
FLIP_FLOPS = 4_000_000_000
SPREAD = 7.0


def call(
    kernel, name, out_shape, in_specs, scratch=(), flops=0, moved=0, limit=VMEM_LIMIT
):
    vmem = pl.BlockSpec(memory_space=pltpu.VMEM)
    return pl.pallas_call(
        kernel,
        name=name,
        out_shape=out_shape,
        in_specs=in_specs,
        out_specs=jax.tree.map(lambda _: vmem, out_shape),
        scratch_shapes=list(scratch),
        compiler_params=pltpu.CompilerParams(vmem_limit_bytes=limit),
        cost_estimate=pl.CostEstimate(flops=flops, bytes_accessed=moved, transcendentals=0),
    )


def in_hbm(array):
    return pltpu.with_memory_space_constraint(array, pltpu.HBM)


def fetch(pairs, sems):
    copies = [
        pltpu.make_async_copy(source, target, sems.at[i])
        for i, (source, target) in enumerate(pairs)
    ]
    for copy in copies:
        copy.start()
    return copies


def pack_kernel(
    state_hbm, lat_hbm, lev_hbm, lat_up, lat_dn, lev_up, lev_dn, state, cour_lat, cour_lev, sems
):
    nlev, nf, nrow, _ = state.shape
    order = [0, nlev - 1] + list(range(1, nlev - 1))
    copies = fetch(
        [(lev_hbm.at[nlev - 1], cour_lev), (lat_hbm, cour_lat)]
        + [(state_hbm.at[level], state.at[level]) for level in order],
        sems,
    )
    copies[0].wait()
    lev_up[nf * nrow :, :] = cour_lev[...].astype(BF)
    copies[1].wait()
    lat_up[nlev * nf :, :] = cour_lat[:, nrow - 1, :].astype(BF)
    for place, level in enumerate(order):
        copies[2 + place].wait()
        rows = slice(level * nf, level * nf + nf)
        block = state[level]
        lat_up[rows, :] = block[:, nrow - 1, :].astype(BF)
        lat_dn[rows, :] = block[:, 0, :].astype(BF)
        if level == 0 or level == nlev - 1:
            target = lev_dn if level == 0 else lev_up
            for field in range(nf):
                target[field * nrow : field * nrow + nrow, :] = block[field].astype(BF)


def interior_kernel(
    ends, state_hbm, lat_hbm, lev_hbm, lon_hbm, part, state, cour_lat, cour_lev, cour_lon, sems
):
    nlev, nf, nrow, nlon = state.shape
    copies = fetch(
        [(lat_hbm, cour_lat), (lev_hbm, cour_lev), (lon_hbm, cour_lon)]
        + [(state_hbm.at[level], state.at[level]) for level in range(nlev)],
        sems,
    )
    for copy in copies[:4]:
        copy.wait()
    row = lax.broadcasted_iota(jnp.int32, (nrow, nlon), 0)
    first_row, last_row = row == 0, row == nrow - 1
    closed_lat = jnp.logical_and(last_row, ends[0] == 1)
    open_lev = jnp.where(ends[1] == 1, 0.0, 1.0).astype(F32)
    for level in range(nlev):
        if level < nlev - 1:
            copies[4 + level].wait()
        n = jnp.where(closed_lat, 0.0, cour_lat[level])
        ns = jnp.where(first_row, 0.0, pltpu.roll(n, 1, 0))
        d = cour_lev[level] * open_lev if level == nlev - 1 else cour_lev[level]
        e = cour_lon[level]
        ew = pltpu.roll(e, 1, 1)
        mid = (
            1.0
            - (jnp.maximum(n, 0.0) - jnp.minimum(ns, 0.0))
            - (jnp.maximum(e, 0.0) - jnp.minimum(ew, 0.0))
            - jnp.maximum(d, 0.0)
        )
        c_n, c_s = jnp.where(last_row, 0.0, jnp.minimum(n, 0.0)), jnp.maximum(ns, 0.0)
        c_e, c_w = jnp.minimum(e, 0.0), jnp.maximum(ew, 0.0)
        c_d = jnp.minimum(d, 0.0)
        if level > 0:
            du = cour_lev[level - 1]
            mid = mid + jnp.minimum(du, 0.0)
            c_u = jnp.maximum(du, 0.0)
        for field in range(nf):
            q = state[level, field]
            t = (
                mid * q
                + (c_s * pltpu.roll(q, 1, 0) - c_n * pltpu.roll(q, nrow - 1, 0))
                + (c_w * pltpu.roll(q, 1, 1) - c_e * pltpu.roll(q, nlon - 1, 1))
            )
            if level > 0:
                t = t + c_u * state[level - 1, field]
            if level < nlev - 1:
                t = t - c_d * state[level + 1, field]
            part[level, field] = t


def edge_kernel(
    part, lat_up, lat_dn, lev_up, lev_dn, from_south, from_north, from_above, from_below,
    moved, sent, south, north, turned,
):
    nlev, nf, nrow, nlon = part.shape
    at = nlev * nf
    south_rate = from_south[at:, :].astype(F32)
    north_rate = lat_up[at:, :].astype(F32)
    for level in range(nlev):
        rows = slice(level * nf, level * nf + nf)
        rate = jnp.broadcast_to(south_rate[level : level + 1], (nf, nlon))
        south[rows, :] = jnp.minimum(rate, 0.0) * lat_dn[rows, :].astype(F32) + jnp.maximum(
            rate, 0.0
        ) * from_south[rows, :].astype(F32)
        rate = jnp.broadcast_to(north_rate[level : level + 1], (nf, nlon))
        north[rows, :] = -jnp.minimum(rate, 0.0) * from_north[rows, :].astype(F32)
    row = lax.broadcasted_iota(jnp.int32, (nrow, nlon), 0)
    first_row, last_row = row == 0, row == nrow - 1
    above_rate = from_above[nf * nrow :, :].astype(F32)
    below_rate = lev_up[nf * nrow :, :].astype(F32)
    u_in, u_out = jnp.maximum(above_rate, 0.0), jnp.minimum(above_rate, 0.0)
    d_in = jnp.minimum(below_rate, 0.0)
    for level in range(nlev):
        for field in range(nf):
            at = level * nf + field
            t = part[level, field] + jnp.where(
                first_row,
                jnp.broadcast_to(south[at : at + 1, :], (nrow, nlon)),
                jnp.where(last_row, jnp.broadcast_to(north[at : at + 1, :], (nrow, nlon)), 0.0),
            )
            rows = slice(field * nrow, field * nrow + nrow)
            if level == 0:
                t = (
                    t
                    + u_out * lev_dn[rows, :].astype(F32)
                    + u_in * from_above[rows, :].astype(F32)
                )
            if level == nlev - 1:
                t = t - d_in * from_below[rows, :].astype(F32)
            moved[level, field] = t
            for half in range(nlon // LANES):
                turned[pl.ds(((level * 2 + half) * nf + field) * nrow, nrow), :] = t[
                    :, half * LANES : half * LANES + LANES
                ]
        for half in range(nlon // LANES):
            for r in range(nrow):
                tile = turned[pl.ds((level * 2 + half) * nf * nrow + r, nf, stride=nrow), :]
                sent[r * 2 + half, level] = jnp.exp2(tile * SPREAD).astype(BF)


def flip_kernel(*refs):
    count = (len(refs) - 1) // 3
    source, target, held = (refs[i * count : i * count + count] for i in range(3))
    copies = fetch(zip(source, held), refs[-1])
    for i in range(count):
        copies[i].wait()

        @pl.loop(0, held[i].shape[0] // 256)
        def _(k, source=held[i], target=target[i]):
            rows = pl.ds(pl.multiple_of(k * 256, 256), 256)
            target[:, rows] = source[rows, :].T


def gelu(x):
    return 0.5 * x * (1.0 + jnp.tanh(0.7978845608028654 * (x + 0.044715 * (x * x * x))))


def column_kernel(
    count, got, remap, in_hbm, out_hbm, rad_hbm, heat_hbm, day, back,
    whole, total, remapped, hidden, rad_part, rad_hidden, w_in, w_out, w_rad, w_heat, sems,
):
    ngroup, nlev, nf, ncol = got.shape
    levels = ngroup * nlev
    copies = fetch(
        [(in_hbm, w_in), (out_hbm, w_out), (rad_hbm, w_rad), (heat_hbm, w_heat)], sems
    )
    w = remap[...]
    high = w.astype(BF)
    low = (w - high.astype(F32)).astype(BF)
    both = jnp.concatenate([high, low], axis=1)
    for group in range(ngroup):
        code = got[group].astype(F32).reshape(nlev * nf, ncol)
        whole[group * nlev * nf : (group + 1) * nlev * nf, :] = jnp.log2(code) * (1.0 / SPREAD)
    for two in range(nf // 2):
        fields = [pl.ds(two * 2 + k, levels, stride=nf) for k in range(2)]
        t = jnp.concatenate([whole[rows, :] for rows in fields], axis=1)
        th = t.astype(BF)
        tl = (t - th.astype(F32)).astype(BF)
        x = t + (
            jnp.dot(both, jnp.concatenate([th, th], axis=0), preferred_element_type=F32)
            + jnp.dot(high, tl, preferred_element_type=F32)
        )
        for k, rows in enumerate(fields):
            total[rows, :] = x[:, k * ncol : k * ncol + ncol]
    chunk = 256
    for i in range(nf * levels // chunk):
        rows = slice(i * chunk, i * chunk + chunk)
        remapped[rows, :] = total[rows, :].astype(BF)

    copies[0].wait()

    @pl.loop(0, w_in.shape[0] // chunk)
    def _(i):
        rows = pl.ds(pl.multiple_of(i * chunk, chunk), chunk)
        hidden[rows, :] = gelu(
            jnp.dot(w_in[rows, :], remapped[...], preferred_element_type=F32)
        ).astype(BF)

    copies[1].wait()

    @pl.loop(0, nf * levels // chunk)
    def _(i):
        rows = pl.ds(pl.multiple_of(i * chunk, chunk), chunk)
        total[rows, :] = total[rows, :] + jnp.dot(
            w_out[rows, :], hidden[...], preferred_element_type=F32
        )

    for field in range(RADF):
        rad_part[pl.ds(field, levels, stride=RADF), :] = total[pl.ds(field, levels, stride=nf), :]
    rad_in = rad_part[...].astype(BF)
    copies[2].wait()
    copies[3].wait()

    for i in range(w_rad.shape[0] // chunk):
        rows = slice(i * chunk, i * chunk + chunk)
        rad_hidden[rows, :] = gelu(
            jnp.dot(w_rad[rows, :], rad_in, preferred_element_type=F32)
        ).astype(BF)

    warm = jnp.dot(w_heat[...], rad_hidden[...], preferred_element_type=F32)
    col = lax.broadcasted_iota(jnp.int32, (ncol, ncol), 0)
    rank = lax.broadcasted_iota(jnp.int32, (ncol, ncol), 1)
    hit = jnp.logical_and(day[...] == col, rank < count[0] * DB)
    lit = lax.dot_general(
        jnp.ones((8, ncol), BF),
        jnp.where(hit, 1.0, 0.0).astype(BF),
        (((1,), (1,)), ((), ())),
        preferred_element_type=F32,
    )
    first = pl.ds(0, levels, stride=nf)
    total[first, :] = total[first, :] + jnp.where(
        jnp.broadcast_to(lit[:1, :], warm.shape) > 0.5, warm, 0.0
    )
    for group in range(ngroup):
        rows = slice(group * nlev * nf, (group + 1) * nlev * nf)
        back[group] = (total[rows, :] - whole[rows, :]).astype(BF).reshape(nlev, nf, ncol)


def finish_kernel(moved, change, out, turned):
    nlev, nf, nrow, nlon = moved.shape
    for level in range(nlev):
        for half in range(nlon // LANES):
            base = (level * 2 + half) * nrow * nf
            for r in range(nrow):
                turned[pl.ds(base + r * nf, nf), :] = change[r * 2 + half, level].astype(F32)
            lanes = slice(half * LANES, half * LANES + LANES)
            for field in range(nf):
                out[level, field, :, lanes] = (
                    moved[level, field, :, lanes] + turned[pl.ds(base + field, nrow, stride=nf), :]
                )


def on_device(
    state, cour_lat, cour_lev, cour_lon, remap_weight, w_in, w_out, w_rad_in,
    radiative_final_weights, day_list, day_count,
):
    nlev, nf, nrow, nlon = state.shape
    nlat_dev, nlev_dev = lax.axis_size("lat"), lax.axis_size("lev")
    levels = nlev * nlev_dev
    ncol = nrow * nlon // nlev_dev
    vmem = pl.BlockSpec(memory_space=pltpu.VMEM)
    smem = pl.BlockSpec(memory_space=pltpu.SMEM)
    hbm = pl.BlockSpec(memory_space=pltpu.HBM)
    shape = jax.ShapeDtypeStruct

    lat_rows, lev_rows = nlev * nf, nf * nrow
    packs = call(
        pack_kernel,
        "pack",
        (
            shape((lat_rows + nlev, nlon), BF),
            shape((lat_rows, nlon), BF),
            shape((lev_rows + nrow, nlon), BF),
            shape((lev_rows, nlon), BF),
        ),
        [hbm] * 3,
        [
            pltpu.VMEM(state.shape, F32),
            pltpu.VMEM(cour_lat.shape, F32),
            pltpu.VMEM(cour_lev.shape[1:], F32),
            pltpu.SemaphoreType.DMA((nlev + 2,)),
        ],
        moved=state.size * 4,
        limit=8 << 20,
    )(*map(in_hbm, (state, cour_lat, cour_lev)))
    lat_up, lat_dn, lev_up, lev_dn = packs
    up_lat = [(i, i + 1) for i in range(nlat_dev - 1)]
    dn_lat = [(i + 1, i) for i in range(nlat_dev - 1)]
    up_lev = [(i, i + 1) for i in range(nlev_dev - 1)]
    dn_lev = [(i + 1, i) for i in range(nlev_dev - 1)]
    from_above = lax.ppermute(lev_up, "lev", up_lev)
    from_below = lax.ppermute(lev_dn, "lev", dn_lev)
    from_south = lax.ppermute(lat_up, "lat", up_lat)
    from_north = lax.ppermute(lat_dn, "lat", dn_lat)

    ends = jnp.stack(
        [lax.axis_index("lat") == nlat_dev - 1, lax.axis_index("lev") == nlev_dev - 1]
    ).astype(jnp.int32)
    part = call(
        interior_kernel,
        "interior",
        shape(state.shape, F32),
        [smem] + [hbm] * 4,
        [pltpu.VMEM(state.shape, F32)]
        + [pltpu.VMEM(cour_lat.shape, F32)] * 3
        + [pltpu.SemaphoreType.DMA((nlev + 3,))],
        flops=state.size * 13,
        moved=state.size * 8,
        limit=8 << 20,
    )(ends, *map(in_hbm, (state, cour_lat, cour_lev, cour_lon)))
    moved, sent = call(
        edge_kernel,
        "edges",
        (shape(state.shape, F32), shape((2 * nrow, nlev, nf, LANES), BF)),
        [vmem] * 9,
        [
            pltpu.VMEM((lat_rows, nlon), F32),
            pltpu.VMEM((lat_rows, nlon), F32),
            pltpu.VMEM((nf * 2 * nlev * nrow, LANES), F32),
        ],
        limit=8 << 20,
    )(part, *packs, from_south, from_north, from_above, from_below)

    got = lax.all_to_all(sent, "lev", split_axis=0, concat_axis=0, tiled=True)

    nhid, nrad = w_in.shape[1], w_rad_in.shape[1]
    weights = (w_in, w_out, w_rad_in, radiative_final_weights)
    flipped = call(
        flip_kernel,
        "flip",
        tuple(shape(w.shape[::-1], BF) for w in weights),
        [hbm] * 4,
        [pltpu.VMEM(w.shape, BF) for w in weights] + [pltpu.SemaphoreType.DMA((4,))],
        flops=FLIP_FLOPS,
        moved=2 * sum(w.size * 2 for w in weights),
        limit=16 << 20,
    )(*map(in_hbm, weights))
    back = call(
        column_kernel,
        "columns",
        shape(got.shape, BF),
        [smem, vmem, vmem, hbm, hbm, hbm, hbm, vmem],
        [
            pltpu.VMEM((nf * levels, ncol), F32),
            pltpu.VMEM((nf * levels, ncol), F32),
            pltpu.VMEM((nf * levels, ncol), BF),
            pltpu.VMEM((nhid, ncol), BF),
            pltpu.VMEM((RADF * levels, ncol), F32),
            pltpu.VMEM((nrad, ncol), BF),
        ]
        + [pltpu.VMEM(w.shape[::-1], BF) for w in weights]
        + [pltpu.SemaphoreType.DMA((4,))],
        limit=20 << 20,
    )(day_count.reshape(1), got, remap_weight, *map(in_hbm, flipped), day_list.reshape(1, -1))

    change = lax.all_to_all(back, "lev", split_axis=0, concat_axis=0, tiled=True)
    return call(
        finish_kernel,
        "finish",
        shape(state.shape, F32),
        [vmem] * 2,
        [pltpu.VMEM((nf * 2 * nlev * nrow, LANES), F32)],
        limit=8 << 20,
    )(moved, change)


def solution(mesh):
    placed = (
        P("lev", None, "lat", None),
        P("lev", "lat", None),
        P("lev", "lat", None),
        P("lev", "lat", None),
        P(),
        P(),
        P(),
        P(),
        P(),
        P("lat", "lev", None),
        P("lat", "lev"),
    )
    return jax.shard_map(
        on_device,
        mesh=mesh,
        in_specs=placed,
        out_specs=P("lev", None, "lat", None),
        check_vma=False,
    )
```

time: 109 us -> 86.6 us (0.79)
  the two profiles are of different devices: /device:TPU:512 before, /device:TPU:388 now
where the time goes in v2:
time: 86.6 us; the launch traced here: 86.3 us
  starting transfers between devices  28.1 us (32%)
  blocking collectives  24.4 us (28%)
  Pallas kernels  18.3 us (21%)
  waiting for transfers between devices  9.66 us (11%)
  local copies, waits for them, and re-layouts  4.99 us (6%)
    all_to_all x1, blocking collectives, on_device(): lax.all_to_all(back, 'lev', split_axis=0, concat_axis=0, tiled=True)  24.4 us
    all_to_all x1, starting transfers between devices, on_device(): got = lax.all_to_all(sent, 'lev', split_axis=0, concat_axis=0, tiled=True)  18.2 us
    all_to_all x1, waiting for transfers between devices, on_device(): got = lax.all_to_all(sent, 'lev', split_axis=0, concat_axis=0, tiled=True)  9.64 us
    pallas_call x1, Pallas kernels, on_device(): call(column_kernel, 'columns', shape(got.shape, BF), [smem, vmem, vmem, h...  6.52 us
    unnamed x12, local copies, waits for them, and re-layouts  4.99 us
    pallas_call x1, Pallas kernels, on_device(): call(flip_kernel, 'flip', tuple((shape(w.shape[::-1], BF) for w in weight...  4.91 us
    ppermute x1, starting transfers between devices, on_device(): from_above = lax.ppermute(lev_up, 'lev', up_lev)  4.27 us
    pallas_call x1, Pallas kernels, on_device(): call(interior_kernel, 'interior', shape(state.shape, F32), [smem] + [hbm]...  2.8 us
  transfers between devices with their start and end apart: 5, of which 1 were waited for; matrix products, arithmetic and copies ran while one was open for 0% of the time, Pallas kernels for 9%

profile of v2, /device:TPU:388, one launch (start us, length us, event | category | flops | bytes accessed | tf_op | source)
XLA Modules:
  0.0 86.3 jit_solution(7675949754965547882)
XLA Ops:
  0.0 1.4 %pack.1 = (bf16[136,256]{1,0:T(8,128)(2,1)S(1)}, bf16[128,256]{1,0:T(8,128)(2,1)S(1)}, bf16[136,256]{1,0:T(8,128)(2,1)S(1)}, bf16[128,256]{1,0:T(8,128)(2,1)S(1)}) custom-call(f32[8,16,8,256]{3,2,1,0:T(8,128)} %state_hbm.3, f32[8,8,256]{2,1,0:T(8,128)} %lat_hbm.3, f32[8,8,256]{2,1,0:T(8,128)} %lev_hbm.3), custom_call_target="tpu_custom_call" | custom-call | bytes 1048576 | tf_op jit(solution)/shard_map/pack/pallas_call | solution.py:300
  1.5 1.9 %collective-permute-start.1 = (bf16[128,256]{1,0:T(8,128)(2,1)S(1)}, bf16[128,256]{1,0:T(8,128)(2,1)S(1)}, u32[]{:S(2)}, u32[]{:S(2)}) collective-permute-start(bf16[128,256]{1,0:T(8,128)(2,1)S(1)} %get-tuple-element.16.lat_dn), channel_id=1, source_target_pairs={{16,0},{32,16},{48,32},{64,48},{80,64},{96,80},{112,96},{128,112},... | collective-permute-start | bytes 196616 | tf_op jit(solution)/shard_map/ppermute | solution.py:327
  3.4 1.3 %collective-permute-start.3 = (bf16[128,256]{1,0:T(8,128)(2,1)S(1)}, bf16[128,256]{1,0:T(8,128)(2,1)S(1)}, u32[]{:S(2)}, u32[]{:S(2)}) collective-permute-start(bf16[128,256]{1,0:T(8,128)(2,1)S(1)} %get-tuple-element.18.lev_dn), channel_id=1, source_target_pairs={{1,0},{2,1},{3,2},{4,3},{5,4},{6,5},{7,6},{8,7},{9,8},{10,9},{11,1... | collective-permute-start | bytes 196616 | tf_op jit(solution)/shard_map/ppermute | solution.py:325
  4.7 2.4 %collective-permute-start = (bf16[136,256]{1,0:T(8,128)(2,1)S(1)}, bf16[136,256]{1,0:T(8,128)(2,1)S(1)}, u32[]{:S(2)}, u32[]{:S(2)}) collective-permute-start(bf16[136,256]{1,0:T(8,128)(2,1)S(1)} %get-tuple-element.15.lat_up), channel_id=1, source_target_pairs={{0,16},{16,32},{32,48},{48,64},{64,80},{80,96},{96,112},{112,128},... | collective-permute-start | bytes 208904 | tf_op jit(solution)/shard_map/ppermute | solution.py:326
  7.1 4.3 %collective-permute-start.2 = (bf16[136,256]{1,0:T(8,128)(2,1)S(1)}, bf16[136,256]{1,0:T(8,128)(2,1)S(1)}, u32[]{:S(2)}, u32[]{:S(2)}) collective-permute-start(bf16[136,256]{1,0:T(8,128)(2,1)S(1)} %get-tuple-element.17.lev_up), channel_id=1, source_target_pairs={{0,1},{1,2},{2,3},{3,4},{4,5},{5,6},{6,7},{7,8},{8,9},{9,10},{10,1... | collective-permute-start | bytes 208904 | tf_op jit(solution)/shard_map/ppermute | solution.py:324
  11.4 0.1 add_convert_fusion.ends
  11.5 2.8 %interior.1.part = f32[8,16,8,256]{3,2,1,0:T(8,128)S(1)} custom-call(s32[2]{0:T(128)S(1)} %add_convert_fusion.ends, f32[8,16,8,256]{3,2,1,0:T(8,128)} %state_hbm.3, f32[8,8,256]{2,1,0:T(8,128)} %lat_hbm.3, f32[8,8,256]{2,1,0:T(8,128)} %lev_hbm.3, f32[8,8,256]{2,1,0:T(8,128)} %lon_hbm.1), custom_call_target="tpu_custom_call" | custom-call | flops 3407872 | bytes 2097152 | tf_op jit(solution)/shard_map/interior/pallas_call | solution.py:332
  14.3 0.0 collective-permute-done.1.from_north
  14.3 0.0 collective-permute-done.3.from_below
  14.3 0.0 collective-permute-done.from_south
  14.3 0.0 collective-permute-done.2.from_above
  14.3 1.2 %edges.1 = (f32[8,16,8,256]{3,2,1,0:T(8,128)S(1)}, bf16[16,8,16,128]{3,2,1,0:T(8,128)(2,1)}) custom-call(f32[8,16,8,256]{3,2,1,0:T(8,128)S(1)} %interior.1.part, bf16[136,256]{1,0:T(8,128)(2,1)S(1)} %get-tuple-element.15.lat_up, bf16[128,256]{1,0:T(8,128)(2,1)S(1)} %get-tuple-element.16.lat_dn, bf16[136,256]{1,0:T(8,128)(2,1)S(1)} %get-tuple-element.17.lev_up, ...), custom_call_target="tpu_custom_call" | custom-call | tf_op jit(solution)/shard_map/edges/pallas_call | solution.py:344
  15.6 18.2 %all-to-all-start = ((bf16[16,8,16,128]{3,2,1,0:T(8,128)(2,1)}), bf16[16,8,16,128]{3,2,1,0:T(8,128)(2,1)S(1)}, u32[]{:S(2)}, u32[]{:S(2)}) async-start(bf16[16,8,16,128]{3,2,1,0:T(8,128)(2,1)} %get-tuple-element.20), calls=%async_computation | async-start | bytes 1048576 | tf_op jit(solution)/shard_map/all_to_all | solution.py:357
  34.4 0.0 copy-start.4
  34.4 0.0 copy-start.5
  34.4 4.9 %flip.1 = (bf16[768,2048]{1,0:T(8,128)(2,1)S(1)}, bf16[2048,768]{1,0:T(8,128)(2,1)S(1)}, bf16[1024,512]{1,0:T(8,128)(2,1)S(1)}, bf16[128,1024]{1,0:T(8,128)(2,1)S(1)}) custom-call(bf16[2048,768]{1,0:T(8,128)(2,1)} %refs_0_.1, bf16[768,2048]{1,0:T(8,128)(2,1)} %refs_1_.1, bf16[512,1024]{1,0:T(8,128)(2,1)} %refs_2_.1, bf16[1024,128]{1,0:T(8,128)(2,1)} %refs_3_.1), custom_call_target="tpu_custom_call" | custom-call | flops 4000000000 | bytes 15204352 | tf_op jit(solution)/shard_map/flip/pallas_call | solution.py:361
  39.3 0.0 copy-start
  39.3 1.6 %copy-done = bf16[768,2048]{1,0:T(8,128)(2,1)} copy-done((bf16[768,2048]{1,0:T(8,128)(2,1)}, bf16[768,2048]{1,0:T(8,128)(2,1)S(1)}, u32[]{:S(2)}) %copy-start) | copy-done | bytes 3145752
  41.0 0.0 copy-start.1
  41.0 1.7 %copy-done.1 = bf16[2048,768]{1,0:T(8,128)(2,1)} copy-done((bf16[2048,768]{1,0:T(8,128)(2,1)}, bf16[2048,768]{1,0:T(8,128)(2,1)S(1)}, u32[]{:S(2)}) %copy-start.1) | copy-done | bytes 3145752
  42.6 0.0 copy-start.2
  42.6 1.0 %copy-done.2 = bf16[1024,512]{1,0:T(8,128)(2,1)} copy-done((bf16[1024,512]{1,0:T(8,128)(2,1)}, bf16[1024,512]{1,0:T(8,128)(2,1)S(1)}, u32[]{:S(2)}) %copy-start.2) | copy-done | bytes 1048600
  43.6 0.0 copy-start.3
  43.6 0.7 copy-done.3
  44.3 9.6 %all-to-all-done.got = bf16[16,8,16,128]{3,2,1,0:T(8,128)(2,1)S(1)} async-done(((bf16[16,8,16,128]{3,2,1,0:T(8,128)(2,1)}), bf16[16,8,16,128]{3,2,1,0:T(8,128)(2,1)S(1)}, u32[]{:S(2)}, u32[]{:S(2)}) %all-to-all-start) | async-done | bytes 524320 | tf_op jit(solution)/shard_map/all_to_all | solution.py:357
  54.0 0.0 copy-done.4
  54.0 0.0 copy-done.5
  54.0 6.5 %columns.1 = bf16[16,8,16,128]{3,2,1,0:T(8,128)(2,1)S(1)} custom-call(s32[1]{0:T(128)} %bitcast.4.count, bf16[16,8,16,128]{3,2,1,0:T(8,128)(2,1)S(1)} %all-to-all-done.got, f32[128,128]{1,0:T(8,128)S(1)} %copy-done.4, bf16[768,2048]{1,0:T(8,128)(2,1)} %copy-done, bf16[2048,768]{1,0:T(8,128)(2,1)} %copy-done.1, bf16[1024,512]{1,0:T(8,128)(2,1)} %copy-done.2, ...), custom_call_target="tpu_custom_call" | custom-call | tf_op jit(solution)/shard_map/columns/pallas_call | solution.py:371
  60.5 24.4 %all_to_all.10.change = bf16[16,8,16,128]{3,2,1,0:T(8,128)(2,1)S(1)} all-to-all(bf16[16,8,16,128]{3,2,1,0:T(8,128)(2,1)S(1)} %columns.1), channel_id=1, replica_groups=mesh['lat'=64,'lev'=16] {'lev'}, dimensions={0} | all-to-all | bytes 1048576 | tf_op jit(solution)/shard_map/all_to_all | solution.py:389
  84.9 1.4 %finish.1 = f32[8,16,8,256]{3,2,1,0:T(8,128)} custom-call(f32[8,16,8,256]{3,2,1,0:T(8,128)S(1)} %get-tuple-element.19.moved, bf16[16,8,16,128]{3,2,1,0:T(8,128)(2,1)S(1)} %all_to_all.10.change), custom_call_target="tpu_custom_call" | custom-call | tf_op jit(solution)/shard_map/finish/pallas_call | solution.py:390
Async XLA Ops:
  1.5 12.8 %collective-permute-start.1 = (bf16[128,256]{1,0:T(8,128)(2,1)S(1)}, bf16[128,256]{1,0:T(8,128)(2,1)S(1)}, u32[]{:S(2)}, u32[]{:S(2)}) collective-permute-start(bf16[128,256]{1,0:T(8,128)(2,1)S(1)} %get-tuple-element.16.lat_dn), channel_id=1, source_target_pairs={{16,0},{32,16},{48,32},{64,48},{80,64},{96,80},{112,96},{128,112},... | collective-permute-start | bytes 196616 | tf_op jit(solution)/shard_map/ppermute | solution.py:327
  3.4 10.9 %collective-permute-start.3 = (bf16[128,256]{1,0:T(8,128)(2,1)S(1)}, bf16[128,256]{1,0:T(8,128)(2,1)S(1)}, u32[]{:S(2)}, u32[]{:S(2)}) collective-permute-start(bf16[128,256]{1,0:T(8,128)(2,1)S(1)} %get-tuple-element.18.lev_dn), channel_id=1, source_target_pairs={{1,0},{2,1},{3,2},{4,3},{5,4},{6,5},{7,6},{8,7},{9,8},{10,9},{11,1... | collective-permute-start | bytes 196616 | tf_op jit(solution)/shard_map/ppermute | solution.py:325
  4.7 9.6 %collective-permute-start = (bf16[136,256]{1,0:T(8,128)(2,1)S(1)}, bf16[136,256]{1,0:T(8,128)(2,1)S(1)}, u32[]{:S(2)}, u32[]{:S(2)}) collective-permute-start(bf16[136,256]{1,0:T(8,128)(2,1)S(1)} %get-tuple-element.15.lat_up), channel_id=1, source_target_pairs={{0,16},{16,32},{32,48},{48,64},{64,80},{80,96},{96,112},{112,128},... | collective-permute-start | bytes 208904 | tf_op jit(solution)/shard_map/ppermute | solution.py:326
  7.1 7.2 %collective-permute-start.2 = (bf16[136,256]{1,0:T(8,128)(2,1)S(1)}, bf16[136,256]{1,0:T(8,128)(2,1)S(1)}, u32[]{:S(2)}, u32[]{:S(2)}) collective-permute-start(bf16[136,256]{1,0:T(8,128)(2,1)S(1)} %get-tuple-element.17.lev_up), channel_id=1, source_target_pairs={{0,1},{1,2},{2,3},{3,4},{4,5},{5,6},{6,7},{7,8},{8,9},{9,10},{10,1... | collective-permute-start | bytes 208904 | tf_op jit(solution)/shard_map/ppermute | solution.py:324
  15.6 38.4 %all-to-all-start = ((bf16[16,8,16,128]{3,2,1,0:T(8,128)(2,1)}), bf16[16,8,16,128]{3,2,1,0:T(8,128)(2,1)S(1)}, u32[]{:S(2)}, u32[]{:S(2)}) async-start(bf16[16,8,16,128]{3,2,1,0:T(8,128)(2,1)} %get-tuple-element.20), calls=%async_computation | async-start | bytes 1048576 | tf_op jit(solution)/shard_map/all_to_all | solution.py:357
  34.4 19.6 %copy-start.4 = (f32[128,128]{1,0:T(8,128)S(1)}, f32[128,128]{1,0:T(8,128)}, u32[]{:S(2)}) copy-start(f32[128,128]{1,0:T(8,128)} %remap.1) | copy-start | bytes 196612
  34.4 19.6 %copy-start.5 = (s32[1,1,128]{2,1,0:T(1,128)S(1)}, s32[1,1,128]{2,1,0:T(1,128)}, u32[]{:S(2)}) copy-start(s32[1,1,128]{2,1,0:T(1,128)} %param.20) | copy-start | bytes 1540
  39.3 1.6 %copy-start = (bf16[768,2048]{1,0:T(8,128)(2,1)}, bf16[768,2048]{1,0:T(8,128)(2,1)S(1)}, u32[]{:S(2)}) copy-start(bf16[768,2048]{1,0:T(8,128)(2,1)S(1)} %get-tuple-element.21.in_hbm) | copy-start | bytes 9437188
  41.0 1.7 %copy-start.1 = (bf16[2048,768]{1,0:T(8,128)(2,1)}, bf16[2048,768]{1,0:T(8,128)(2,1)S(1)}, u32[]{:S(2)}) copy-start(bf16[2048,768]{1,0:T(8,128)(2,1)S(1)} %get-tuple-element.22.out_hbm) | copy-start | bytes 9437188
  42.6 1.0 %copy-start.2 = (bf16[1024,512]{1,0:T(8,128)(2,1)}, bf16[1024,512]{1,0:T(8,128)(2,1)S(1)}, u32[]{:S(2)}) copy-start(bf16[1024,512]{1,0:T(8,128)(2,1)S(1)} %get-tuple-element.23.rad_hbm) | copy-start | bytes 3145732
  43.6 0.7 copy-start.3

commit v3 on v2

v3 whole, which is shorter than its diff:
```python
import jax
import jax.numpy as jnp
from jax import lax
from jax.experimental import pallas as pl
from jax.experimental.pallas import tpu as pltpu
from jax.sharding import PartitionSpec as P

RADF = 4
DB = 16
LANES = 128
BLOCK = 256
BF = jnp.bfloat16
F32 = jnp.float32
VMEM_LIMIT = 16 << 20
FLIP_FLOPS = 4_000_000_000
SPREAD = 7.0


def call(
    kernel, name, out_shape, in_specs, scratch=(), flops=0, moved=0, limit=VMEM_LIMIT, out_specs=None
):
    vmem = pl.BlockSpec(memory_space=pltpu.VMEM)
    return pl.pallas_call(
        kernel,
        name=name,
        out_shape=out_shape,
        in_specs=in_specs,
        out_specs=out_specs or jax.tree.map(lambda _: vmem, out_shape),
        scratch_shapes=list(scratch),
        compiler_params=pltpu.CompilerParams(vmem_limit_bytes=limit),
        cost_estimate=pl.CostEstimate(flops=flops, bytes_accessed=moved, transcendentals=0),
    )


def in_hbm(array):
    return pltpu.with_memory_space_constraint(array, pltpu.HBM)


def fetch(pairs, sems):
    copies = [
        pltpu.make_async_copy(source, target, sems.at[i])
        for i, (source, target) in enumerate(pairs)
    ]
    for copy in copies:
        copy.start()
    return copies


def pack_kernel(
    ends, state_hbm, lat_hbm, lev_hbm, lat_pair, lat_other, lev_pair, lev_other,
    state, cour_lat, cour_lev, both, sems,
):
    nlev, nf, nrow, _ = state.shape
    order = [0, nlev - 1] + list(range(1, nlev - 1))
    copies = fetch(
        [(lev_hbm.at[nlev - 1], cour_lev), (lat_hbm, cour_lat)]
        + [(state_hbm.at[level], state.at[level]) for level in order],
        sems,
    )
    copies[0].wait()
    lev_pair[nf * nrow :, :] = cour_lev[...].astype(BF)
    lev_other[nf * nrow :, :] = cour_lev[...].astype(BF)
    copies[1].wait()
    rates = cour_lat[:, nrow - 1, :].astype(BF)
    lat_pair[nlev * nf :, :] = rates
    lat_other[nlev * nf :, :] = rates
    copies[2].wait()
    copies[3].wait()
    odd = ends[3]
    for field in range(nf):
        rows = slice(field * nrow, field * nrow + nrow)
        lev_pair[rows, :] = state[(1 - odd) * (nlev - 1), field].astype(BF)
        lev_other[rows, :] = state[odd * (nlev - 1), field].astype(BF)
    for place, level in enumerate(order):
        if place > 1:
            copies[2 + place].wait()
        rows = slice(level * nf, level * nf + nf)
        block = state[level]
        both[0, rows, :] = block[:, nrow - 1, :].astype(BF)
        both[1, rows, :] = block[:, 0, :].astype(BF)
    lat_pair[: nlev * nf, :] = both[ends[2]]
    lat_other[: nlev * nf, :] = both[1 - ends[2]]


def interior_kernel(
    ends, state_hbm, lat_hbm, lev_hbm, lon_hbm, part, state, cour_lat, cour_lev, cour_lon, sems
):
    nlev, nf, nrow, nlon = state.shape
    copies = fetch(
        [(lat_hbm, cour_lat), (lev_hbm, cour_lev), (lon_hbm, cour_lon)]
        + [(state_hbm.at[level], state.at[level]) for level in range(nlev)],
        sems,
    )
    for copy in copies[:4]:
        copy.wait()
    row = lax.broadcasted_iota(jnp.int32, (nrow, nlon), 0)
    first_row, last_row = row == 0, row == nrow - 1
    closed_lat = jnp.logical_and(last_row, ends[0] == 1)
    open_lev = jnp.where(ends[1] == 1, 0.0, 1.0).astype(F32)
    for level in range(nlev):
        if level < nlev - 1:
            copies[4 + level].wait()
        n = jnp.where(closed_lat, 0.0, cour_lat[level])
        ns = jnp.where(first_row, 0.0, pltpu.roll(n, 1, 0))
        d = cour_lev[level] * open_lev if level == nlev - 1 else cour_lev[level]
        e = cour_lon[level]
        ew = pltpu.roll(e, 1, 1)
        mid = (
            1.0
            - (jnp.maximum(n, 0.0) - jnp.minimum(ns, 0.0))
            - (jnp.maximum(e, 0.0) - jnp.minimum(ew, 0.0))
            - jnp.maximum(d, 0.0)
        )
        c_n, c_s = jnp.where(last_row, 0.0, jnp.minimum(n, 0.0)), jnp.maximum(ns, 0.0)
        c_e, c_w = jnp.minimum(e, 0.0), jnp.maximum(ew, 0.0)
        c_d = jnp.minimum(d, 0.0)
        if level > 0:
            du = cour_lev[level - 1]
            mid = mid + jnp.minimum(du, 0.0)
            c_u = jnp.maximum(du, 0.0)
        for field in range(nf):
            q = state[level, field]
            t = (
                mid * q
                + (c_s * pltpu.roll(q, 1, 0) - c_n * pltpu.roll(q, nrow - 1, 0))
                + (c_w * pltpu.roll(q, 1, 1) - c_e * pltpu.roll(q, nlon - 1, 1))
            )
            if level > 0:
                t = t + c_u * state[level - 1, field]
            if level < nlev - 1:
                t = t - c_d * state[level + 1, field]
            part[level, field] = t


def edge_kernel(
    ends, part, lat_pair, lat_other, lev_pair, lev_other,
    from_lat_pair, from_lat_other, from_lev_pair, from_lev_other,
    moved, sent, south, north, turned,
):
    nlev, nf, nrow, nlon = part.shape
    lat_odd, lev_odd = ends[2] == 1, ends[3] == 1

    def pick(odd, rows, if_odd, if_even):
        return jnp.where(odd, if_odd[rows, :].astype(F32), if_even[rows, :].astype(F32))

    tail = slice(nlev * nf, nlev * nf + nlev)
    south_rate = pick(lat_odd, tail, from_lat_pair, from_lat_other)
    north_rate = lat_pair[tail, :].astype(F32)
    for level in range(nlev):
        rows = slice(level * nf, level * nf + nf)
        rate = jnp.broadcast_to(south_rate[level : level + 1], (nf, nlon))
        south[rows, :] = jnp.minimum(rate, 0.0) * pick(
            lat_odd, rows, lat_pair, lat_other
        ) + jnp.maximum(rate, 0.0) * pick(lat_odd, rows, from_lat_pair, from_lat_other)
        rate = jnp.broadcast_to(north_rate[level : level + 1], (nf, nlon))
        north[rows, :] = -jnp.minimum(rate, 0.0) * pick(
            lat_odd, rows, from_lat_other, from_lat_pair
        )
    row = lax.broadcasted_iota(jnp.int32, (nrow, nlon), 0)
    first_row, last_row = row == 0, row == nrow - 1
    tail = slice(nf * nrow, nf * nrow + nrow)
    above_rate = pick(lev_odd, tail, from_lev_pair, from_lev_other)
    below_rate = lev_pair[tail, :].astype(F32)
    u_in, u_out = jnp.maximum(above_rate, 0.0), jnp.minimum(above_rate, 0.0)
    d_in = jnp.minimum(below_rate, 0.0)
    for field in range(nf):
        for level in range(nlev):
            at = level * nf + field
            t = part[level, field] + jnp.where(
                first_row,
                jnp.broadcast_to(south[at : at + 1, :], (nrow, nlon)),
                jnp.where(last_row, jnp.broadcast_to(north[at : at + 1, :], (nrow, nlon)), 0.0),
            )
            rows = slice(field * nrow, field * nrow + nrow)
            if level == 0:
                t = (
                    t
                    + u_out * pick(lev_odd, rows, lev_pair, lev_other)
                    + u_in * pick(lev_odd, rows, from_lev_pair, from_lev_other)
                )
            if level == nlev - 1:
                t = t - d_in * pick(lev_odd, rows, from_lev_other, from_lev_pair)
            moved[level, field] = t
            for half in range(nlon // LANES):
                turned[pl.ds(((field * 2 + half) * nlev + level) * nrow, nrow), :] = t[
                    :, half * LANES : half * LANES + LANES
                ]
        for half in range(nlon // LANES):
            for r in range(nrow):
                tile = turned[pl.ds((field * 2 + half) * nlev * nrow + r, nlev, stride=nrow), :]
                sent[r * 2 + half, field] = jnp.exp2(tile * SPREAD).astype(BF)


def swap_rows(rows, inner):
    to = lax.broadcasted_iota(jnp.int32, (rows, rows), 0)
    source = lax.broadcasted_iota(jnp.int32, (rows, rows), 1)
    outer = rows // inner
    wanted = lax.rem(to, outer) * inner + lax.div(to, outer)
    return jnp.where(source == wanted, 1.0, 0.0).astype(BF)


def flip_kernel(
    in_hbm, out_hbm, rad_hbm, heat_hbm, in_t_hbm, out_t_hbm, rad_t_hbm, heat_t_hbm,
    w_in, w_out, w_rad, w_heat, in_t, out_t, rad_t, heat_t, perm, sems, out_sems,
):
    copies = fetch([(in_hbm, w_in), (out_hbm, w_out), (rad_hbm, w_rad), (heat_hbm, w_heat)], sems)
    perm[...] = swap_rows(BLOCK, BLOCK // 16)
    results = []

    def done(source, target):
        results.append(pltpu.make_async_copy(source, target, out_sems.at[len(results)]))
        results[-1].start()

    copies[0].wait()

    @pl.loop(0, w_in.shape[0] // BLOCK)
    def _(k):
        rows = pl.ds(pl.multiple_of(k * BLOCK, BLOCK), BLOCK)
        in_t[:, rows] = (
            jnp.dot(perm[...], w_in[rows, :], preferred_element_type=F32).astype(BF).T
        )

    done(in_t, in_t_hbm)
    copies[1].wait()

    @pl.loop(0, w_out.shape[1] // BLOCK)
    def _(k):
        rows = pl.ds(pl.multiple_of(k * BLOCK, BLOCK), BLOCK)
        out_t[rows, :] = jnp.dot(
            perm[...], w_out[:, rows].T, preferred_element_type=F32
        ).astype(BF)

    done(out_t, out_t_hbm)
    perm[...] = swap_rows(BLOCK, RADF)
    copies[2].wait()
    for k in range(w_rad.shape[0] // BLOCK):
        rows = slice(k * BLOCK, k * BLOCK + BLOCK)
        rad_t[:, rows] = (
            jnp.dot(perm[...], w_rad[rows, :], preferred_element_type=F32).astype(BF).T
        )
    done(rad_t, rad_t_hbm)
    copies[3].wait()
    heat_t[...] = w_heat[...].T
    done(heat_t, heat_t_hbm)
    for copy in results:
        copy.wait()


def gelu(x):
    return 0.5 * x * (1.0 + jnp.tanh(0.7978845608028654 * (x + 0.044715 * (x * x * x))))


def column_kernel(
    count, got, remap, in_hbm, out_hbm, rad_hbm, heat_hbm, day, back,
    whole, total, remapped, hidden, rad_in, rad_hidden, w_in, w_out, w_rad, w_heat, sems,
):
    copies = fetch(
        [(in_hbm, w_in), (out_hbm, w_out), (rad_hbm, w_rad), (heat_hbm, w_heat)], sems
    )
    ngroup, nf, nlev, ncol = got.shape
    levels = ngroup * nlev
    deep = BLOCK // nf
    w = remap[...]
    high = w.astype(BF)
    low = (w - high.astype(F32)).astype(BF)
    both = jnp.concatenate([high, low], axis=1)
    for two in range(nf // 2):
        ts = []
        for k in range(2):
            field = two * 2 + k
            code = got[:, field].astype(F32).reshape(levels, ncol)
            ts.append(jnp.log2(code) * (1.0 / SPREAD))
            whole[field * levels : field * levels + levels, :] = ts[-1]
        t = jnp.concatenate(ts, axis=1)
        th = t.astype(BF)
        tl = (t - th.astype(F32)).astype(BF)
        x = t + (
            jnp.dot(both, jnp.concatenate([th, th], axis=0), preferred_element_type=F32)
            + jnp.dot(high, tl, preferred_element_type=F32)
        )
        for k in range(2):
            for block in range(levels // deep):
                at = block * BLOCK + (two * 2 + k) * deep
                tile = x[block * deep : block * deep + deep, k * ncol : k * ncol + ncol]
                total[at : at + deep, :] = tile
                remapped[at : at + deep, :] = tile.astype(BF)
    copies[0].wait()
    for i in range(w_in.shape[0] // BLOCK):
        rows = slice(i * BLOCK, i * BLOCK + BLOCK)
        hidden[rows, :] = gelu(
            jnp.dot(w_in[rows, :], remapped[...], preferred_element_type=F32)
        ).astype(BF)
    copies[1].wait()
    blocks_each = levels // deep // (w_rad.shape[1] // BLOCK)
    for i in range(nf * levels // BLOCK):
        rows = slice(i * BLOCK, i * BLOCK + BLOCK)
        total[rows, :] = total[rows, :] + jnp.dot(
            w_out[rows, :], hidden[...], preferred_element_type=F32
        )
        for field in range(RADF):
            at = (i // blocks_each) * BLOCK + (field * blocks_each + i % blocks_each) * deep
            first = i * BLOCK + field * deep
            rad_in[at : at + deep, :] = total[first : first + deep, :].astype(BF)
    copies[2].wait()
    copies[3].wait()
    for i in range(w_rad.shape[0] // BLOCK):
        rows = slice(i * BLOCK, i * BLOCK + BLOCK)
        rad_hidden[rows, :] = gelu(
            jnp.dot(w_rad[rows, :], rad_in[...], preferred_element_type=F32)
        ).astype(BF)
    for field in range(1, nf):
        for group in range(ngroup):
            at = (group * nlev // deep) * BLOCK + field * deep + group * nlev % deep
            own = field * levels + group * nlev
            back[group, field] = (total[at : at + nlev, :] - whole[own : own + nlev, :]).astype(BF)
    warm = jnp.dot(w_heat[...], rad_hidden[...], preferred_element_type=F32)
    col = lax.broadcasted_iota(jnp.int32, (ncol, ncol), 0)
    rank = lax.broadcasted_iota(jnp.int32, (ncol, ncol), 1)
    hit = jnp.logical_and(day[...] == col, rank < count[0] * DB)
    lit = lax.dot_general(
        jnp.ones((8, ncol), BF),
        jnp.where(hit, 1.0, 0.0).astype(BF),
        (((1,), (1,)), ((), ())),
        preferred_element_type=F32,
    )
    warm = jnp.where(jnp.broadcast_to(lit[:1, :], warm.shape) > 0.5, warm, 0.0)
    for group in range(ngroup):
        at = (group * nlev // deep) * BLOCK + group * nlev % deep
        own = group * nlev
        back[group, 0] = (
            total[at : at + nlev, :] - whole[own : own + nlev, :] + warm[own : own + nlev, :]
        ).astype(BF)


def finish_kernel(moved, change, out, turned):
    nlev, nf, nrow, nlon = moved.shape
    for field in range(nf):
        for half in range(nlon // LANES):
            base = (field * 2 + half) * nrow * nlev
            for r in range(nrow):
                turned[pl.ds(base + r * nlev, nlev), :] = change[r * 2 + half, field].astype(F32)
            lanes = slice(half * LANES, half * LANES + LANES)
            for level in range(nlev):
                out[level, field, :, lanes] = (
                    moved[level, field, :, lanes]
                    + turned[pl.ds(base + level, nrow, stride=nlev), :]
                )


def on_device(
    state, cour_lat, cour_lev, cour_lon, remap_weight, w_in, w_out, w_rad_in,
    radiative_final_weights, day_list, day_count,
):
    nlev, nf, nrow, nlon = state.shape
    nlat_dev, nlev_dev = lax.axis_size("lat"), lax.axis_size("lev")
    levels = nlev * nlev_dev
    ncol = nrow * nlon // nlev_dev
    vmem = pl.BlockSpec(memory_space=pltpu.VMEM)
    smem = pl.BlockSpec(memory_space=pltpu.SMEM)
    hbm = pl.BlockSpec(memory_space=pltpu.HBM)
    shape = jax.ShapeDtypeStruct

    lat_rows, lev_rows = nlev * nf, nf * nrow
    lat_at, lev_at = lax.axis_index("lat"), lax.axis_index("lev")
    ends = jnp.stack(
        [lat_at == nlat_dev - 1, lev_at == nlev_dev - 1, lat_at & 1 == 1, lev_at & 1 == 1]
    ).astype(jnp.int32)
    packs = call(
        pack_kernel,
        "pack",
        (shape((lat_rows + nlev, nlon), BF),) * 2 + (shape((lev_rows + nrow, nlon), BF),) * 2,
        [smem] + [hbm] * 3,
        [
            pltpu.VMEM(state.shape, F32),
            pltpu.VMEM(cour_lat.shape, F32),
            pltpu.VMEM(cour_lev.shape[1:], F32),
            pltpu.VMEM((2, lat_rows, nlon), BF),
            pltpu.SemaphoreType.DMA((nlev + 2,)),
        ],
        moved=state.size * 4,
        limit=8 << 20,
    )(ends, *map(in_hbm, (state, cour_lat, cour_lev)))

    def trade(value, axis, count, first):
        pairs = [(i, i + 1) for i in range(first, count - 1, 2)]
        return lax.ppermute(value, axis, pairs + [(j, i) for i, j in pairs])

    halos = [
        trade(packs[0], "lat", nlat_dev, 0),
        trade(packs[1], "lat", nlat_dev, 1),
        trade(packs[2], "lev", nlev_dev, 0),
        trade(packs[3], "lev", nlev_dev, 1),
    ]
    part = call(
        interior_kernel,
        "interior",
        shape(state.shape, F32),
        [smem] + [hbm] * 4,
        [pltpu.VMEM(state.shape, F32)]
        + [pltpu.VMEM(cour_lat.shape, F32)] * 3
        + [pltpu.SemaphoreType.DMA((nlev + 3,))],
        flops=state.size * 13,
        moved=state.size * 8,
        limit=8 << 20,
    )(ends, *map(in_hbm, (state, cour_lat, cour_lev, cour_lon)))
    moved, sent = call(
        edge_kernel,
        "edges",
        (shape(state.shape, F32), shape((2 * nrow, nf, nlev, LANES), BF)),
        [smem] + [vmem] * 9,
        [
            pltpu.VMEM((lat_rows, nlon), F32),
            pltpu.VMEM((lat_rows, nlon), F32),
            pltpu.VMEM((nf * 2 * nlev * nrow, LANES), F32),
        ],
        limit=8 << 20,
    )(ends, part, *packs, *halos)

    got = lax.all_to_all(sent, "lev", split_axis=0, concat_axis=0, tiled=True)

    nhid, nrad = w_in.shape[1], w_rad_in.shape[1]
    weights = (w_in, w_out, w_rad_in, radiative_final_weights)
    flipped = call(
        flip_kernel,
        "flip",
        tuple(pltpu.HBM(w.shape[::-1], BF) for w in weights),
        [hbm] * 4,
        [pltpu.VMEM(w.shape, BF) for w in weights]
        + [pltpu.VMEM(w.shape[::-1], BF) for w in weights]
        + [pltpu.VMEM((BLOCK, BLOCK), BF)]
        + [pltpu.SemaphoreType.DMA((4,))] * 2,
        flops=FLIP_FLOPS,
        moved=2 * sum(w.size * 2 for w in weights),
        limit=20 << 20,
        out_specs=(hbm,) * 4,
    )(*map(in_hbm, weights))
    back = call(
        column_kernel,
        "columns",
        shape(got.shape, BF),
        [smem, vmem, vmem, hbm, hbm, hbm, hbm, vmem],
        [
            pltpu.VMEM((nf * levels, ncol), F32),
            pltpu.VMEM((nf * levels, ncol), F32),
            pltpu.VMEM((nf * levels, ncol), BF),
            pltpu.VMEM((nhid, ncol), BF),
            pltpu.VMEM((RADF * levels, ncol), BF),
            pltpu.VMEM((nrad, ncol), BF),
        ]
        + [pltpu.VMEM(w.shape[::-1], BF) for w in weights]
        + [pltpu.SemaphoreType.DMA((4,))],
        limit=20 << 20,
    )(day_count.reshape(1), got, remap_weight, *map(in_hbm, flipped), day_list.reshape(1, -1))

    change = lax.all_to_all(back, "lev", split_axis=0, concat_axis=0, tiled=True)
    return call(
        finish_kernel,
        "finish",
        shape(state.shape, F32),
        [vmem] * 2,
        [pltpu.VMEM((nf * 2 * nlev * nrow, LANES), F32)],
        limit=8 << 20,
    )(moved, change)


def solution(mesh):
    placed = (
        P("lev", None, "lat", None),
        P("lev", "lat", None),
        P("lev", "lat", None),
        P("lev", "lat", None),
        P(),
        P(),
        P(),
        P(),
        P(),
        P("lat", "lev", None),
        P("lat", "lev"),
    )
    return jax.shard_map(
        on_device,
        mesh=mesh,
        in_specs=placed,
        out_specs=P("lev", None, "lat", None),
        check_vma=False,
    )
```

time: 86.6 us -> 82.3 us (0.950)
  the two profiles are of different devices: /device:TPU:388 before, /device:TPU:4 now
where the time goes in v3:
time: 82.3 us; the launch traced here: 81.9 us
  blocking collectives  24.1 us (29%)
  starting transfers between devices  23.8 us (29%)
  Pallas kernels  22.2 us (27%)
  waiting for transfers between devices  10.9 us (13%)
    all_to_all x1, blocking collectives, on_device(): lax.all_to_all(back, 'lev', split_axis=0, concat_axis=0, tiled=True)  24.1 us
    all_to_all x1, starting transfers between devices, on_device(): got = lax.all_to_all(sent, 'lev', split_axis=0, concat_axis=0, tiled=True)  15.1 us
    all_to_all x1, waiting for transfers between devices, on_device(): got = lax.all_to_all(sent, 'lev', split_axis=0, concat_axis=0, tiled=True)  10.9 us
    pallas_call x1, Pallas kernels, on_device(): call(flip_kernel, 'flip', tuple((pltpu.HBM(w.shape[::-1], BF) for w in we...  9.35 us
    ppermute x4, starting transfers between devices, trade(): return lax.ppermute(value, axis, pairs + [(j, i) for i, j in pairs])  8.73 us
    pallas_call x1, Pallas kernels, on_device(): call(column_kernel, 'columns', shape(got.shape, BF), [smem, vmem, vmem, h...  4.89 us
    pallas_call x1, Pallas kernels, on_device(): call(interior_kernel, 'interior', shape(state.shape, F32), [smem] + [hbm]...  2.8 us
    pallas_call x1, Pallas kernels, on_device(): call(pack_kernel, 'pack', (shape((lat_rows + nlev, nlon), BF),) * 2 + (sh...  2 us
  transfers between devices with their start and end apart: 5, of which 1 were waited for; matrix products, arithmetic and copies ran while one was open for 0% of the time, Pallas kernels for 15%

profile of v3, /device:TPU:4, one launch (start us, length us, event | category | flops | bytes accessed | tf_op | source)
XLA Modules:
  0.0 81.9 jit_solution(15833998193937619803)
XLA Ops:
  0.0 0.1 add_convert_fusion.ends
  0.1 2.0 %pack.1 = (bf16[136,256]{1,0:T(8,128)(2,1)S(1)}, bf16[136,256]{1,0:T(8,128)(2,1)S(1)}, bf16[136,256]{1,0:T(8,128)(2,1)S(1)}, bf16[136,256]{1,0:T(8,128)(2,1)S(1)}) custom-call(s32[4]{0:T(128)S(1)} %add_convert_fusion.ends, f32[8,16,8,256]{3,2,1,0:T(8,128)} %state_hbm.3, f32[8,8,256]{2,1,0:T(8,128)} %lat_hbm.3, f32[8,8,256]{2,1,0:T(8,128)} %lev_hbm.3), custom_call_target="tpu_custom_call" | custom-call | bytes 1048576 | tf_op jit(solution)/shard_map/pack/pallas_call | solution.py:368
  2.1 1.9 %collective-permute-start = (bf16[136,256]{1,0:T(8,128)(2,1)S(1)}, bf16[136,256]{1,0:T(8,128)(2,1)S(1)}, u32[]{:S(2)}, u32[]{:S(2)}) collective-permute-start(bf16[136,256]{1,0:T(8,128)(2,1)S(1)} %get-tuple-element.15.lat_pair), channel_id=1, source_target_pairs={{0,16},{32,48},{64,80},{96,112},{128,144},{160,176},{192,208},{224... | collective-permute-start | bytes 208904 | tf_op jit(solution)/shard_map/ppermute | solution.py:386
  4.0 2.5 %collective-permute-start.1 = (bf16[136,256]{1,0:T(8,128)(2,1)S(1)}, bf16[136,256]{1,0:T(8,128)(2,1)S(1)}, u32[]{:S(2)}, u32[]{:S(2)}) collective-permute-start(bf16[136,256]{1,0:T(8,128)(2,1)S(1)} %get-tuple-element.16.lat_other), channel_id=1, source_target_pairs={{16,32},{48,64},{80,96},{112,128},{144,160},{176,192},{208,224},{2... | collective-permute-start | bytes 208904 | tf_op jit(solution)/shard_map/ppermute | solution.py:386
  6.6 3.6 %collective-permute-start.2 = (bf16[136,256]{1,0:T(8,128)(2,1)S(1)}, bf16[136,256]{1,0:T(8,128)(2,1)S(1)}, u32[]{:S(2)}, u32[]{:S(2)}) collective-permute-start(bf16[136,256]{1,0:T(8,128)(2,1)S(1)} %get-tuple-element.17.lev_pair), channel_id=1, source_target_pairs={{0,1},{2,3},{4,5},{6,7},{8,9},{10,11},{12,13},{14,15},{1,0},{3,2},... | collective-permute-start | bytes 208904 | tf_op jit(solution)/shard_map/ppermute | solution.py:386
  10.2 0.7 collective-permute-start.3
  10.8 2.8 %interior.1.part = f32[8,16,8,256]{3,2,1,0:T(8,128)S(1)} custom-call(s32[4]{0:T(128)S(1)} %add_convert_fusion.ends, f32[8,16,8,256]{3,2,1,0:T(8,128)} %state_hbm.3, f32[8,8,256]{2,1,0:T(8,128)} %lat_hbm.3, f32[8,8,256]{2,1,0:T(8,128)} %lev_hbm.3, f32[8,8,256]{2,1,0:T(8,128)} %lon_hbm.1), custom_call_target="tpu_custom_call" | custom-call | flops 3407872 | bytes 2097152 | tf_op jit(solution)/shard_map/interior/pallas_call | solution.py:394
  13.7 0.0 collective-permute-done.from_lat_pair
  13.7 0.0 collective-permute-done.1.from_lat_other
  13.7 0.0 collective-permute-done.2.from_lev_pair
  13.7 0.0 collective-permute-done.3.from_lev_other
  13.7 1.9 %edges.1 = (f32[8,16,8,256]{3,2,1,0:T(8,128)S(1)}, bf16[16,16,8,128]{3,2,1,0:T(8,128)(2,1)}) custom-call(s32[4]{0:T(128)S(1)} %add_convert_fusion.ends, f32[8,16,8,256]{3,2,1,0:T(8,128)S(1)} %interior.1.part, bf16[136,256]{1,0:T(8,128)(2,1)S(1)} %get-tuple-element.15.lat_pair, bf16[136,256]{1,0:T(8,128)(2,1)S(1)} %get-tuple-element.16.lat_other, ...), custom_call_target="tpu_custom_call" | custom-call | tf_op jit(solution)/shard_map/edges/pallas_call | solution.py:406
  15.6 15.1 %all-to-all-start = ((bf16[16,16,8,128]{3,2,1,0:T(8,128)(2,1)}), bf16[16,16,8,128]{3,2,1,0:T(8,128)(2,1)S(1)}, u32[]{:S(2)}, u32[]{:S(2)}) async-start(bf16[16,16,8,128]{3,2,1,0:T(8,128)(2,1)} %get-tuple-element.20), calls=%async_computation | async-start | bytes 1048576 | tf_op jit(solution)/shard_map/all_to_all | solution.py:419
  31.4 0.0 copy-start
  31.4 0.0 copy-start.1
  31.4 9.3 %flip.1 = (bf16[768,2048]{1,0:T(8,128)(2,1)}, bf16[2048,768]{1,0:T(8,128)(2,1)}, bf16[1024,512]{1,0:T(8,128)(2,1)}, bf16[128,1024]{1,0:T(8,128)(2,1)}) custom-call(bf16[2048,768]{1,0:T(8,128)(2,1)} %in_hbm.1, bf16[768,2048]{1,0:T(8,128)(2,1)} %out_hbm.1, bf16[512,1024]{1,0:T(8,128)(2,1)} %rad_hbm.1, bf16[1024,128]{1,0:T(8,128)(2,1)} %heat_hbm.1), custom_call_target="tpu_custom_call" | custom-call | flops 4000000000 | bytes 15204352 | tf_op jit(solution)/shard_map/flip/pallas_call | solution.py:423
  40.8 10.9 %all-to-all-done.got = bf16[16,16,8,128]{3,2,1,0:T(8,128)(2,1)S(1)} async-done(((bf16[16,16,8,128]{3,2,1,0:T(8,128)(2,1)}), bf16[16,16,8,128]{3,2,1,0:T(8,128)(2,1)S(1)}, u32[]{:S(2)}, u32[]{:S(2)}) %all-to-all-start) | async-done | bytes 524320 | tf_op jit(solution)/shard_map/all_to_all | solution.py:419
  51.7 0.0 copy-done
  51.7 0.0 copy-done.1
  51.7 4.9 %columns.1 = bf16[16,16,8,128]{3,2,1,0:T(8,128)(2,1)S(1)} custom-call(s32[1]{0:T(128)} %bitcast.6.count, bf16[16,16,8,128]{3,2,1,0:T(8,128)(2,1)S(1)} %all-to-all-done.got, f32[128,128]{1,0:T(8,128)S(1)} %copy-done, bf16[768,2048]{1,0:T(8,128)(2,1)} %get-tuple-element.21.in_hbm, bf16[2048,768]{1,0:T(8,128)(2,1)} %get-tuple-element.22.out_hbm, ...), custom_call_target="tpu_custom_call" | custom-call | tf_op jit(solution)/shard_map/columns/pallas_call | solution.py:437
  56.6 24.1 %all_to_all.10.change = bf16[16,16,8,128]{3,2,1,0:T(8,128)(2,1)S(1)} all-to-all(bf16[16,16,8,128]{3,2,1,0:T(8,128)(2,1)S(1)} %columns.1), channel_id=1, replica_groups=mesh['lat'=64,'lev'=16] {'lev'}, dimensions={0} | all-to-all | bytes 1048576 | tf_op jit(solution)/shard_map/all_to_all | solution.py:455
  80.7 1.3 %finish.1 = f32[8,16,8,256]{3,2,1,0:T(8,128)} custom-call(f32[8,16,8,256]{3,2,1,0:T(8,128)S(1)} %get-tuple-element.19.moved, bf16[16,16,8,128]{3,2,1,0:T(8,128)(2,1)S(1)} %all_to_all.10.change), custom_call_target="tpu_custom_call" | custom-call | tf_op jit(solution)/shard_map/finish/pallas_call | solution.py:456
Async XLA Ops:
  2.1 11.6 %collective-permute-start = (bf16[136,256]{1,0:T(8,128)(2,1)S(1)}, bf16[136,256]{1,0:T(8,128)(2,1)S(1)}, u32[]{:S(2)}, u32[]{:S(2)}) collective-permute-start(bf16[136,256]{1,0:T(8,128)(2,1)S(1)} %get-tuple-element.15.lat_pair), channel_id=1, source_target_pairs={{0,16},{32,48},{64,80},{96,112},{128,144},{160,176},{192,208},{224... | collective-permute-start | bytes 208904 | tf_op jit(solution)/shard_map/ppermute | solution.py:386
  4.0 9.7 %collective-permute-start.1 = (bf16[136,256]{1,0:T(8,128)(2,1)S(1)}, bf16[136,256]{1,0:T(8,128)(2,1)S(1)}, u32[]{:S(2)}, u32[]{:S(2)}) collective-permute-start(bf16[136,256]{1,0:T(8,128)(2,1)S(1)} %get-tuple-element.16.lat_other), channel_id=1, source_target_pairs={{16,32},{48,64},{80,96},{112,128},{144,160},{176,192},{208,224},{2... | collective-permute-start | bytes 208904 | tf_op jit(solution)/shard_map/ppermute | solution.py:386
  6.6 7.1 %collective-permute-start.2 = (bf16[136,256]{1,0:T(8,128)(2,1)S(1)}, bf16[136,256]{1,0:T(8,128)(2,1)S(1)}, u32[]{:S(2)}, u32[]{:S(2)}) collective-permute-start(bf16[136,256]{1,0:T(8,128)(2,1)S(1)} %get-tuple-element.17.lev_pair), channel_id=1, source_target_pairs={{0,1},{2,3},{4,5},{6,7},{8,9},{10,11},{12,13},{14,15},{1,0},{3,2},... | collective-permute-start | bytes 208904 | tf_op jit(solution)/shard_map/ppermute | solution.py:386
  10.2 3.5 %collective-permute-start.3 = (bf16[136,256]{1,0:T(8,128)(2,1)S(1)}, bf16[136,256]{1,0:T(8,128)(2,1)S(1)}, u32[]{:S(2)}, u32[]{:S(2)}) collective-permute-start(bf16[136,256]{1,0:T(8,128)(2,1)S(1)} %get-tuple-element.18.lev_other), channel_id=1, source_target_pairs={{1,2},{3,4},{5,6},{7,8},{9,10},{11,12},{13,14},{2,1},{4,3},{6,5},{... | collective-permute-start | bytes 208904 | tf_op jit(solution)/shard_map/ppermute | solution.py:386
  15.6 36.1 %all-to-all-start = ((bf16[16,16,8,128]{3,2,1,0:T(8,128)(2,1)}), bf16[16,16,8,128]{3,2,1,0:T(8,128)(2,1)S(1)}, u32[]{:S(2)}, u32[]{:S(2)}) async-start(bf16[16,16,8,128]{3,2,1,0:T(8,128)(2,1)} %get-tuple-element.20), calls=%async_computation | async-start | bytes 1048576 | tf_op jit(solution)/shard_map/all_to_all | solution.py:419
  31.4 20.3 %copy-start = (f32[128,128]{1,0:T(8,128)S(1)}, f32[128,128]{1,0:T(8,128)}, u32[]{:S(2)}) copy-start(f32[128,128]{1,0:T(8,128)} %remap.1) | copy-start | bytes 196612
  31.4 20.3 %copy-start.1 = (s32[1,1,128]{2,1,0:T(1,128)S(1)}, s32[1,1,128]{2,1,0:T(1,128)}, u32[]{:S(2)}) copy-start(s32[1,1,128]{2,1,0:T(1,128)} %param.20) | copy-start | bytes 1540

commit v4 on v3

--- a/solution.py
+++ b/solution.py
@@ -9,6 +9,7 @@
 DB = 16
 LANES = 128
 BLOCK = 256
+SOME = 4
 BF = jnp.bfloat16
 F32 = jnp.float32
 VMEM_LIMIT = 16 << 20
@@ -47,26 +48,28 @@
 
 
 def pack_kernel(
-    ends, state_hbm, lat_hbm, lev_hbm, lat_pair, lat_other, lev_pair, lev_other,
-    state, cour_lat, cour_lev, both, sems,
+    state_hbm, lat_hbm, lev_hbm, lon_hbm, lat_pair, lat_other, lev_pair, lev_other,
+    state, cour_lat, cour_lev, cour_lon, both, sems,
 ):
     nlev, nf, nrow, _ = state.shape
     order = [0, nlev - 1] + list(range(1, nlev - 1))
     copies = fetch(
-        [(lev_hbm.at[nlev - 1], cour_lev), (lat_hbm, cour_lat)]
-        + [(state_hbm.at[level], state.at[level]) for level in order],
+        [(lev_hbm, cour_lev), (lat_hbm, cour_lat)]
+        + [(state_hbm.at[level], state.at[level]) for level in order]
+        + [(lon_hbm, cour_lon)],
         sems,
     )
     copies[0].wait()
-    lev_pair[nf * nrow :, :] = cour_lev[...].astype(BF)
-    lev_other[nf * nrow :, :] = cour_lev[...].astype(BF)
+    lev_pair[nf * nrow :, :] = cour_lev[nlev - 1].astype(BF)
+    lev_other[nf * nrow :, :] = cour_lev[nlev - 1].astype(BF)
     copies[1].wait()
     rates = cour_lat[:, nrow - 1, :].astype(BF)
     lat_pair[nlev * nf :, :] = rates
     lat_other[nlev * nf :, :] = rates
     copies[2].wait()
     copies[3].wait()
-    odd = ends[3]
+    odd = lax.axis_index("lev") & 1
+    lat_odd = lax.axis_index("lat") & 1
     for field in range(nf):
         rows = slice(field * nrow, field * nrow + nrow)
         lev_pair[rows, :] = state[(1 - odd) * (nlev - 1), field].astype(BF)
@@ -78,28 +81,20 @@
         block = state[level]
         both[0, rows, :] = block[:, nrow - 1, :].astype(BF)
         both[1, rows, :] = block[:, 0, :].astype(BF)
-    lat_pair[: nlev * nf, :] = both[ends[2]]
-    lat_other[: nlev * nf, :] = both[1 - ends[2]]
-
-
-def interior_kernel(
-    ends, state_hbm, lat_hbm, lev_hbm, lon_hbm, part, state, cour_lat, cour_lev, cour_lon, sems
-):
+    lat_pair[: nlev * nf, :] = both[lat_odd]
+    lat_other[: nlev * nf, :] = both[1 - lat_odd]
+    copies[-1].wait()
+
+
+def interior_kernel(state, cour_lat, cour_lev, cour_lon, part):
     nlev, nf, nrow, nlon = state.shape
-    copies = fetch(
-        [(lat_hbm, cour_lat), (lev_hbm, cour_lev), (lon_hbm, cour_lon)]
-        + [(state_hbm.at[level], state.at[level]) for level in range(nlev)],
-        sems,
-    )
-    for copy in copies[:4]:
-        copy.wait()
+    last_lat = lax.axis_index("lat") == lax.axis_size("lat") - 1
+    last_lev = lax.axis_index("lev") == lax.axis_size("lev") - 1
     row = lax.broadcasted_iota(jnp.int32, (nrow, nlon), 0)
     first_row, last_row = row == 0, row == nrow - 1
-    closed_lat = jnp.logical_and(last_row, ends[0] == 1)
-    open_lev = jnp.where(ends[1] == 1, 0.0, 1.0).astype(F32)
+    closed_lat = jnp.logical_and(last_row, last_lat)
+    open_lev = jnp.where(last_lev, 0.0, 1.0).astype(F32)
     for level in range(nlev):
-        if level < nlev - 1:
-            copies[4 + level].wait()
         n = jnp.where(closed_lat, 0.0, cour_lat[level])
         ns = jnp.where(first_row, 0.0, pltpu.roll(n, 1, 0))
         d = cour_lev[level] * open_lev if level == nlev - 1 else cour_lev[level]
@@ -133,12 +128,12 @@
 
 
 def edge_kernel(
-    ends, part, lat_pair, lat_other, lev_pair, lev_other,
+    part, lat_pair, lat_other, lev_pair, lev_other,
     from_lat_pair, from_lat_other, from_lev_pair, from_lev_other,
-    moved, sent, south, north, turned,
+    moved, sent_hbm, south, north, turned, sent, sems,
 ):
     nlev, nf, nrow, nlon = part.shape
-    lat_odd, lev_odd = ends[2] == 1, ends[3] == 1
+    lat_odd, lev_odd = lax.axis_index("lat") & 1 == 1, lax.axis_index("lev") & 1 == 1
 
     def pick(odd, rows, if_odd, if_even):
         return jnp.where(odd, if_odd[rows, :].astype(F32), if_even[rows, :].astype(F32))
@@ -163,6 +158,7 @@
     below_rate = lev_pair[tail, :].astype(F32)
     u_in, u_out = jnp.maximum(above_rate, 0.0), jnp.minimum(above_rate, 0.0)
     d_in = jnp.minimum(below_rate, 0.0)
+    copies = []
     for field in range(nf):
         for level in range(nlev):
             at = level * nf + field
@@ -189,6 +185,11 @@
             for r in range(nrow):
                 tile = turned[pl.ds((field * 2 + half) * nlev * nrow + r, nlev, stride=nrow), :]
                 sent[r * 2 + half, field] = jnp.exp2(tile * SPREAD).astype(BF)
+        if (field + 1) % SOME == 0:
+            put = slice(field + 1 - SOME, field + 1)
+            copies += fetch([(sent.at[:, put], sent_hbm.at[:, put])], sems.at[field // SOME])
+    for copy in copies:
+        copy.wait()
 
 
 def swap_rows(rows, inner):
@@ -316,7 +317,7 @@
     warm = jnp.dot(w_heat[...], rad_hidden[...], preferred_element_type=F32)
     col = lax.broadcasted_iota(jnp.int32, (ncol, ncol), 0)
     rank = lax.broadcasted_iota(jnp.int32, (ncol, ncol), 1)
-    hit = jnp.logical_and(day[...] == col, rank < count[0] * DB)
+    hit = jnp.logical_and(day[...] == col, rank < count[0, 0] * DB)
     lit = lax.dot_general(
         jnp.ones((8, ncol), BF),
         jnp.where(hit, 1.0, 0.0).astype(BF),
@@ -332,8 +333,9 @@
         ).astype(BF)
 
 
-def finish_kernel(moved, change, out, turned):
+def finish_kernel(moved, change, out_hbm, turned, out, sems):
     nlev, nf, nrow, nlon = moved.shape
+    copies = []
     for field in range(nf):
         for half in range(nlon // LANES):
             base = (field * 2 + half) * nrow * nlev
@@ -345,6 +347,11 @@
                     moved[level, field, :, lanes]
                     + turned[pl.ds(base + level, nrow, stride=nlev), :]
                 )
+        if (field + 1) % SOME == 0:
+            put = slice(field + 1 - SOME, field + 1)
+            copies += fetch([(out.at[:, put], out_hbm.at[:, put])], sems.at[field // SOME])
+    for copy in copies:
+        copy.wait()
 
 
 def on_device(
@@ -356,30 +363,26 @@
     levels = nlev * nlev_dev
     ncol = nrow * nlon // nlev_dev
     vmem = pl.BlockSpec(memory_space=pltpu.VMEM)
-    smem = pl.BlockSpec(memory_space=pltpu.SMEM)
     hbm = pl.BlockSpec(memory_space=pltpu.HBM)
     shape = jax.ShapeDtypeStruct
 
     lat_rows, lev_rows = nlev * nf, nf * nrow
-    lat_at, lev_at = lax.axis_index("lat"), lax.axis_index("lev")
-    ends = jnp.stack(
-        [lat_at == nlat_dev - 1, lev_at == nlev_dev - 1, lat_at & 1 == 1, lev_at & 1 == 1]
-    ).astype(jnp.int32)
     packs = call(
         pack_kernel,
         "pack",
-        (shape((lat_rows + nlev, nlon), BF),) * 2 + (shape((lev_rows + nrow, nlon), BF),) * 2,
-        [smem] + [hbm] * 3,
+        (shape((lat_rows + nlev, nlon), BF),) * 2
+        + (shape((lev_rows + nrow, nlon), BF),) * 2
+        + (shape(state.shape, F32),)
+        + (shape(cour_lat.shape, F32),) * 3,
+        [hbm] * 4,
         [
-            pltpu.VMEM(state.shape, F32),
-            pltpu.VMEM(cour_lat.shape, F32),
-            pltpu.VMEM(cour_lev.shape[1:], F32),
             pltpu.VMEM((2, lat_rows, nlon), BF),
-            pltpu.SemaphoreType.DMA((nlev + 2,)),
+            pltpu.SemaphoreType.DMA((nlev + 3,)),
         ],
         moved=state.size * 4,
         limit=8 << 20,
-    )(ends, *map(in_hbm, (state, cour_lat, cour_lev)))
+    )(*map(in_hbm, (state, cour_lat, cour_lev, cour_lon)))
+    packs, held = packs[:4], packs[4:]
 
     def trade(value, axis, count, first):
         pairs = [(i, i + 1) for i in range(first, count - 1, 2)]
@@ -395,26 +398,26 @@
         interior_kernel,
         "interior",
         shape(state.shape, F32),
-        [smem] + [hbm] * 4,
-        [pltpu.VMEM(state.shape, F32)]
-        + [pltpu.VMEM(cour_lat.shape, F32)] * 3
-        + [pltpu.SemaphoreType.DMA((nlev + 3,))],
+        [vmem] * 4,
         flops=state.size * 13,
         moved=state.size * 8,
         limit=8 << 20,
-    )(ends, *map(in_hbm, (state, cour_lat, cour_lev, cour_lon)))
+    )(*held)
     moved, sent = call(
         edge_kernel,
         "edges",
-        (shape(state.shape, F32), shape((2 * nrow, nf, nlev, LANES), BF)),
-        [smem] + [vmem] * 9,
+        (shape(state.shape, F32), pltpu.HBM((2 * nrow, nf, nlev, LANES), BF)),
+        [vmem] * 9,
         [
             pltpu.VMEM((lat_rows, nlon), F32),
             pltpu.VMEM((lat_rows, nlon), F32),
             pltpu.VMEM((nf * 2 * nlev * nrow, LANES), F32),
+            pltpu.VMEM((2 * nrow, nf, nlev, LANES), BF),
+            pltpu.SemaphoreType.DMA((nf // SOME, 1)),
         ],
         limit=8 << 20,
-    )(ends, part, *packs, *halos)
+        out_specs=(vmem, hbm),
+    )(part, *packs, *halos)
 
     got = lax.all_to_all(sent, "lev", split_axis=0, concat_axis=0, tiled=True)
 
@@ -438,7 +441,7 @@
         column_kernel,
         "columns",
         shape(got.shape, BF),
-        [smem, vmem, vmem, hbm, hbm, hbm, hbm, vmem],
+        [pl.BlockSpec(memory_space=pltpu.SMEM)] + [vmem] * 2 + [hbm] * 4 + [vmem],
         [
             pltpu.VMEM((nf * levels, ncol), F32),
             pltpu.VMEM((nf * levels, ncol), F32),
@@ -450,16 +453,21 @@
         + [pltpu.VMEM(w.shape[::-1], BF) for w in weights]
         + [pltpu.SemaphoreType.DMA((4,))],
         limit=20 << 20,
-    )(day_count.reshape(1), got, remap_weight, *map(in_hbm, flipped), day_list.reshape(1, -1))
+    )(day_count, got, remap_weight, *map(in_hbm, flipped), day_list.reshape(1, -1))
 
     change = lax.all_to_all(back, "lev", split_axis=0, concat_axis=0, tiled=True)
     return call(
         finish_kernel,
         "finish",
-        shape(state.shape, F32),
+        pltpu.HBM(state.shape, F32),
         [vmem] * 2,
-        [pltpu.VMEM((nf * 2 * nlev * nrow, LANES), F32)],
+        [
+            pltpu.VMEM((nf * 2 * nlev * nrow, LANES), F32),
+            pltpu.VMEM(state.shape, F32),
+            pltpu.SemaphoreType.DMA((nf // SOME, 1)),
+        ],
         limit=8 << 20,
+        out_specs=hbm,
     )(moved, change)
 
 

time: 82.3 us -> 80.8 us (0.982)
  Pallas kernels: 22.2 us -> 18.7 us
  waiting for transfers between devices: 10.9 us -> 12.8 us
    pallas_call x4, Pallas kernels: 10.9 us -> 7.94 us  [the longest x1 4.88 us: on_device(): call(column_kernel, 'columns', shape(got.shape, BF), [pl.BlockSpec(memory...]
    ppermute x4, waiting for transfers between devices: 0.01 us -> 1.92 us  [trade(): return lax.ppermute(value, axis, pairs + [(j, i) for i, j in pairs])]
  transfers between devices with their start and end apart: 5 -> 5, of which waited for: 1 -> 2; matrix products, arithmetic and copies ran while one was open for 0% -> 0% of each run, Pallas kernels for 15% -> 13%
where the time goes in v4:
time: 80.8 us; the launch traced here: 80.4 us
  blocking collectives  24.1 us (30%)
  starting transfers between devices  24 us (30%)
  Pallas kernels  18.7 us (23%)
  waiting for transfers between devices  12.8 us (16%)
    all_to_all x1, blocking collectives, on_device(): lax.all_to_all(back, 'lev', split_axis=0, concat_axis=0, tiled=True)  24.1 us
    all_to_all x1, starting transfers between devices, on_device(): got = lax.all_to_all(sent, 'lev', split_axis=0, concat_axis=0, tiled=True)  15.3 us
    all_to_all x1, waiting for transfers between devices, on_device(): got = lax.all_to_all(sent, 'lev', split_axis=0, concat_axis=0, tiled=True)  10.9 us
    pallas_call x1, Pallas kernels, on_device(): call(flip_kernel, 'flip', tuple((pltpu.HBM(w.shape[::-1], BF) for w in we...  9.35 us
    ppermute x4, starting transfers between devices, trade(): return lax.ppermute(value, axis, pairs + [(j, i) for i, j in pairs])  8.73 us
    pallas_call x1, Pallas kernels, on_device(): call(column_kernel, 'columns', shape(got.shape, BF), [pl.BlockSpec(memory...  4.88 us
    ppermute x4, waiting for transfers between devices, trade(): return lax.ppermute(value, axis, pairs + [(j, i) for i, j in pairs])  1.92 us
  transfers between devices with their start and end apart: 5, of which 2 were waited for; matrix products, arithmetic and copies ran while one was open for 0% of the time, Pallas kernels for 13%

profile of v4, /device:TPU:4, one launch (start us, length us, event | category | flops | bytes accessed | tf_op | source)
XLA Modules:
  0.0 80.4 jit_solution(12917197688961275478)
XLA Ops:
  0.0 1.5 %pack.1 = (bf16[136,256]{1,0:T(8,128)(2,1)S(1)}, bf16[136,256]{1,0:T(8,128)(2,1)S(1)}, bf16[136,256]{1,0:T(8,128)(2,1)S(1)}, bf16[136,256]{1,0:T(8,128)(2,1)S(1)...) custom-call(f32[8,16,8,256]{3,2,1,0:T(8,128)} %state_hbm.1, ...), custom_call_target="tpu_custom_call" | custom-call | bytes 1048576 | tf_op jit(solution)/shard_map/pack/pallas_call | solution.py:370
  1.5 1.9 %collective-permute-start = (bf16[136,256]{1,0:T(8,128)(2,1)S(1)}, bf16[136,256]{1,0:T(8,128)(2,1)S(1)}, u32[]{:S(2)}, u32[]{:S(2)}) collective-permute-start(bf16[136,256]{1,0:T(8,128)(2,1)S(1)} %get-tuple-element.23.lat_pair), channel_id=1, source_target_pairs={{0,16},{32,48},{64,80},{96,112},{128,144},{160,176},{192,208},{224... | collective-permute-start | bytes 208904 | tf_op jit(solution)/shard_map/ppermute | solution.py:389
  3.4 2.5 %collective-permute-start.1 = (bf16[136,256]{1,0:T(8,128)(2,1)S(1)}, bf16[136,256]{1,0:T(8,128)(2,1)S(1)}, u32[]{:S(2)}, u32[]{:S(2)}) collective-permute-start(bf16[136,256]{1,0:T(8,128)(2,1)S(1)} %get-tuple-element.24.lat_other), channel_id=1, source_target_pairs={{16,32},{48,64},{80,96},{112,128},{144,160},{176,192},{208,224},{2... | collective-permute-start | bytes 208904 | tf_op jit(solution)/shard_map/ppermute | solution.py:389
  5.9 3.6 %collective-permute-start.2 = (bf16[136,256]{1,0:T(8,128)(2,1)S(1)}, bf16[136,256]{1,0:T(8,128)(2,1)S(1)}, u32[]{:S(2)}, u32[]{:S(2)}) collective-permute-start(bf16[136,256]{1,0:T(8,128)(2,1)S(1)} %get-tuple-element.25.lev_pair), channel_id=1, source_target_pairs={{0,1},{2,3},{4,5},{6,7},{8,9},{10,11},{12,13},{14,15},{1,0},{3,2},... | collective-permute-start | bytes 208904 | tf_op jit(solution)/shard_map/ppermute | solution.py:389
  9.6 0.7 collective-permute-start.3
  10.2 0.7 interior.1.part
  11.0 0.0 collective-permute-done.from_lat_pair
  11.0 0.0 collective-permute-done.1.from_lat_other
  11.0 1.9 %collective-permute-done.2.from_lev_pair = bf16[136,256]{1,0:T(8,128)(2,1)S(1)} collective-permute-done((bf16[136,256]{1,0:T(8,128)(2,1)S(1)}, bf16[136,256]{1,0:T(8,128)(2,1)S(1)}, u32[]{:S(2)}, u32[]{:S(2)}) %collective-permute-start.2) | collective-permute-done | bytes 69664 | tf_op jit(solution)/shard_map/ppermute | solution.py:389
  12.9 0.0 collective-permute-done.3.from_lev_other
  12.9 1.3 %edges.1 = (f32[8,16,8,256]{3,2,1,0:T(8,128)S(1)}, bf16[16,16,8,128]{3,2,1,0:T(8,128)(2,1)}) custom-call(f32[8,16,8,256]{3,2,1,0:T(8,128)S(1)} %interior.1.part, bf16[136,256]{1,0:T(8,128)(2,1)S(1)} %get-tuple-element.23.lat_pair, bf16[136,256]{1,0:T(8,128)(2,1)S(1)} %get-tuple-element.24.lat_other, bf16[136,256]{1,0:T(8,128)(2,1)S(1)} %get-tuple-element.25.lev_pair, ...), custom_call_target="tpu_custom_call" | custom-call | tf_op jit(solution)/shard_map/edges/pallas_call | solution.py:406
  14.2 15.3 %all-to-all-start = ((bf16[16,16,8,128]{3,2,1,0:T(8,128)(2,1)}), bf16[16,16,8,128]{3,2,1,0:T(8,128)(2,1)S(1)}, u32[]{:S(2)}, u32[]{:S(2)}) async-start(bf16[16,16,8,128]{3,2,1,0:T(8,128)(2,1)} %get-tuple-element.28), calls=%async_computation | async-start | bytes 1048576 | tf_op jit(solution)/shard_map/all_to_all | solution.py:422
  30.1 0.0 copy-start
  30.1 0.0 copy-start.1
  30.1 9.3 %flip.1 = (bf16[768,2048]{1,0:T(8,128)(2,1)}, bf16[2048,768]{1,0:T(8,128)(2,1)}, bf16[1024,512]{1,0:T(8,128)(2,1)}, bf16[128,1024]{1,0:T(8,128)(2,1)}) custom-call(bf16[2048,768]{1,0:T(8,128)(2,1)} %in_hbm.1, bf16[768,2048]{1,0:T(8,128)(2,1)} %out_hbm.1, bf16[512,1024]{1,0:T(8,128)(2,1)} %rad_hbm.1, bf16[1024,128]{1,0:T(8,128)(2,1)} %heat_hbm.1), custom_call_target="tpu_custom_call" | custom-call | flops 4000000000 | bytes 15204352 | tf_op jit(solution)/shard_map/flip/pallas_call | solution.py:426
  39.5 10.9 %all-to-all-done.got = bf16[16,16,8,128]{3,2,1,0:T(8,128)(2,1)S(1)} async-done(((bf16[16,16,8,128]{3,2,1,0:T(8,128)(2,1)}), bf16[16,16,8,128]{3,2,1,0:T(8,128)(2,1)S(1)}, u32[]{:S(2)}, u32[]{:S(2)}) %all-to-all-start) | async-done | bytes 524320 | tf_op jit(solution)/shard_map/all_to_all | solution.py:422
  50.4 0.0 copy-done
  50.4 0.0 copy-done.1
  50.4 4.9 %columns.1 = bf16[16,16,8,128]{3,2,1,0:T(8,128)(2,1)S(1)} custom-call(s32[1,1]{1,0:T(1,128)S(6)} %copy.12.count, bf16[16,16,8,128]{3,2,1,0:T(8,128)(2,1)S(1)} %all-to-all-done.got, f32[128,128]{1,0:T(8,128)S(1)} %copy-done, bf16[768,2048]{1,0:T(8,128)(2,1)} %get-tuple-element.29.in_hbm, bf16[2048,768]{1,0:T(8,128)(2,1)} %get-tuple-element.30.out_hbm, ...), custom_call_target="tpu_custom_call" | custom-call | tf_op jit(solution)/shard_map/columns/pallas_call | solution.py:440
  55.3 24.1 %all_to_all.10.change = bf16[16,16,8,128]{3,2,1,0:T(8,128)(2,1)S(1)} all-to-all(bf16[16,16,8,128]{3,2,1,0:T(8,128)(2,1)S(1)} %columns.1), channel_id=1, replica_groups=mesh['lat'=64,'lev'=16] {'lev'}, dimensions={0} | all-to-all | bytes 1048576 | tf_op jit(solution)/shard_map/all_to_all | solution.py:458
  79.4 1.1 %finish.1 = f32[8,16,8,256]{3,2,1,0:T(8,128)} custom-call(f32[8,16,8,256]{3,2,1,0:T(8,128)S(1)} %get-tuple-element.27.moved, bf16[16,16,8,128]{3,2,1,0:T(8,128)(2,1)S(1)} %all_to_all.10.change), custom_call_target="tpu_custom_call" | custom-call | tf_op jit(solution)/shard_map/finish/pallas_call | solution.py:459
Async XLA Ops:
  1.5 9.5 %collective-permute-start = (bf16[136,256]{1,0:T(8,128)(2,1)S(1)}, bf16[136,256]{1,0:T(8,128)(2,1)S(1)}, u32[]{:S(2)}, u32[]{:S(2)}) collective-permute-start(bf16[136,256]{1,0:T(8,128)(2,1)S(1)} %get-tuple-element.23.lat_pair), channel_id=1, source_target_pairs={{0,16},{32,48},{64,80},{96,112},{128,144},{160,176},{192,208},{224... | collective-permute-start | bytes 208904 | tf_op jit(solution)/shard_map/ppermute | solution.py:389
  3.4 7.6 %collective-permute-start.1 = (bf16[136,256]{1,0:T(8,128)(2,1)S(1)}, bf16[136,256]{1,0:T(8,128)(2,1)S(1)}, u32[]{:S(2)}, u32[]{:S(2)}) collective-permute-start(bf16[136,256]{1,0:T(8,128)(2,1)S(1)} %get-tuple-element.24.lat_other), channel_id=1, source_target_pairs={{16,32},{48,64},{80,96},{112,128},{144,160},{176,192},{208,224},{2... | collective-permute-start | bytes 208904 | tf_op jit(solution)/shard_map/ppermute | solution.py:389
  5.9 6.9 %collective-permute-start.2 = (bf16[136,256]{1,0:T(8,128)(2,1)S(1)}, bf16[136,256]{1,0:T(8,128)(2,1)S(1)}, u32[]{:S(2)}, u32[]{:S(2)}) collective-permute-start(bf16[136,256]{1,0:T(8,128)(2,1)S(1)} %get-tuple-element.25.lev_pair), channel_id=1, source_target_pairs={{0,1},{2,3},{4,5},{6,7},{8,9},{10,11},{12,13},{14,15},{1,0},{3,2},... | collective-permute-start | bytes 208904 | tf_op jit(solution)/shard_map/ppermute | solution.py:389
  9.6 3.3 %collective-permute-start.3 = (bf16[136,256]{1,0:T(8,128)(2,1)S(1)}, bf16[136,256]{1,0:T(8,128)(2,1)S(1)}, u32[]{:S(2)}, u32[]{:S(2)}) collective-permute-start(bf16[136,256]{1,0:T(8,128)(2,1)S(1)} %get-tuple-element.26.lev_other), channel_id=1, source_target_pairs={{1,2},{3,4},{5,6},{7,8},{9,10},{11,12},{13,14},{2,1},{4,3},{6,5},{... | collective-permute-start | bytes 208904 | tf_op jit(solution)/shard_map/ppermute | solution.py:389
  14.2 36.2 %all-to-all-start = ((bf16[16,16,8,128]{3,2,1,0:T(8,128)(2,1)}), bf16[16,16,8,128]{3,2,1,0:T(8,128)(2,1)S(1)}, u32[]{:S(2)}, u32[]{:S(2)}) async-start(bf16[16,16,8,128]{3,2,1,0:T(8,128)(2,1)} %get-tuple-element.28), calls=%async_computation | async-start | bytes 1048576 | tf_op jit(solution)/shard_map/all_to_all | solution.py:422
  30.1 20.2 %copy-start = (f32[128,128]{1,0:T(8,128)S(1)}, f32[128,128]{1,0:T(8,128)}, u32[]{:S(2)}) copy-start(f32[128,128]{1,0:T(8,128)} %remap.1) | copy-start | bytes 196612
  30.1 20.2 %copy-start.1 = (s32[1,1,128]{2,1,0:T(1,128)S(1)}, s32[1,1,128]{2,1,0:T(1,128)}, u32[]{:S(2)}) copy-start(s32[1,1,128]{2,1,0:T(1,128)} %param.20) | copy-start | bytes 1540

commit v5 on v4

--- a/solution.py
+++ b/solution.py
@@ -255,9 +255,11 @@
     count, got, remap, in_hbm, out_hbm, rad_hbm, heat_hbm, day, back,
     whole, total, remapped, hidden, rad_in, rad_hidden, w_in, w_out, w_rad, w_heat, sems,
 ):
-    copies = fetch(
-        [(in_hbm, w_in), (out_hbm, w_out), (rad_hbm, w_rad), (heat_hbm, w_heat)], sems
-    )
+    pieces = []
+    for source, target in ((in_hbm, w_in), (out_hbm, w_out), (rad_hbm, w_rad)):
+        for at in range(0, source.shape[0], BLOCK):
+            pieces.append((source.at[at : at + BLOCK], target.at[at : at + BLOCK]))
+    copies = iter(fetch(pieces + [(heat_hbm, w_heat)], sems))
     ngroup, nf, nlev, ncol = got.shape
     levels = ngroup * nlev
     deep = BLOCK // nf
@@ -285,15 +287,15 @@
                 tile = x[block * deep : block * deep + deep, k * ncol : k * ncol + ncol]
                 total[at : at + deep, :] = tile
                 remapped[at : at + deep, :] = tile.astype(BF)
-    copies[0].wait()
     for i in range(w_in.shape[0] // BLOCK):
+        next(copies).wait()
         rows = slice(i * BLOCK, i * BLOCK + BLOCK)
         hidden[rows, :] = gelu(
             jnp.dot(w_in[rows, :], remapped[...], preferred_element_type=F32)
         ).astype(BF)
-    copies[1].wait()
     blocks_each = levels // deep // (w_rad.shape[1] // BLOCK)
     for i in range(nf * levels // BLOCK):
+        next(copies).wait()
         rows = slice(i * BLOCK, i * BLOCK + BLOCK)
         total[rows, :] = total[rows, :] + jnp.dot(
             w_out[rows, :], hidden[...], preferred_element_type=F32
@@ -302,9 +304,8 @@
             at = (i // blocks_each) * BLOCK + (field * blocks_each + i % blocks_each) * deep
             first = i * BLOCK + field * deep
             rad_in[at : at + deep, :] = total[first : first + deep, :].astype(BF)
-    copies[2].wait()
-    copies[3].wait()
     for i in range(w_rad.shape[0] // BLOCK):
+        next(copies).wait()
         rows = slice(i * BLOCK, i * BLOCK + BLOCK)
         rad_hidden[rows, :] = gelu(
             jnp.dot(w_rad[rows, :], rad_in[...], preferred_element_type=F32)
@@ -314,6 +315,7 @@
             at = (group * nlev // deep) * BLOCK + field * deep + group * nlev % deep
             own = field * levels + group * nlev
             back[group, field] = (total[at : at + nlev, :] - whole[own : own + nlev, :]).astype(BF)
+    next(copies).wait()
     warm = jnp.dot(w_heat[...], rad_hidden[...], preferred_element_type=F32)
     col = lax.broadcasted_iota(jnp.int32, (ncol, ncol), 0)
     rank = lax.broadcasted_iota(jnp.int32, (ncol, ncol), 1)
@@ -451,7 +453,7 @@
             pltpu.VMEM((nrad, ncol), BF),
         ]
         + [pltpu.VMEM(w.shape[::-1], BF) for w in weights]
-        + [pltpu.SemaphoreType.DMA((4,))],
+        + [pltpu.SemaphoreType.DMA(((nhid + nf * levels + nrad) // BLOCK + 1,))],
         limit=20 << 20,
     )(day_count, got, remap_weight, *map(in_hbm, flipped), day_list.reshape(1, -1))
 

time: 80.8 us -> 82.4 us (1.020)
  Pallas kernels: 18.7 us -> 20.4 us
    pallas_call x1, Pallas kernels: 4.88 us -> 6.5 us  [on_device(): call(column_kernel, 'columns', shape(got.shape, BF), [pl.BlockSpec(memory...]
  transfers between devices with their start and end apart: 5 -> 5, of which waited for: 2 -> 2; matrix products, arithmetic and copies ran while one was open for 0% -> 0% of each run, Pallas kernels for 13% -> 12%
where the time goes in v5:
time: 82.4 us; the launch traced here: 82.1 us
  blocking collectives  24.1 us (29%)
  starting transfers between devices  24 us (29%)
  Pallas kernels  20.4 us (25%)
  waiting for transfers between devices  12.8 us (16%)
    all_to_all x1, blocking collectives, on_device(): lax.all_to_all(back, 'lev', split_axis=0, concat_axis=0, tiled=True)  24.1 us
    all_to_all x1, starting transfers between devices, on_device(): got = lax.all_to_all(sent, 'lev', split_axis=0, concat_axis=0, tiled=True)  15.3 us
    all_to_all x1, waiting for transfers between devices, on_device(): got = lax.all_to_all(sent, 'lev', split_axis=0, concat_axis=0, tiled=True)  10.9 us
    pallas_call x1, Pallas kernels, on_device(): call(flip_kernel, 'flip', tuple((pltpu.HBM(w.shape[::-1], BF) for w in we...  9.35 us
    ppermute x4, starting transfers between devices, trade(): return lax.ppermute(value, axis, pairs + [(j, i) for i, j in pairs])  8.73 us
    pallas_call x1, Pallas kernels, on_device(): call(column_kernel, 'columns', shape(got.shape, BF), [pl.BlockSpec(memory...  6.5 us
    ppermute x4, waiting for transfers between devices, trade(): return lax.ppermute(value, axis, pairs + [(j, i) for i, j in pairs])  1.92 us
  transfers between devices with their start and end apart: 5, of which 2 were waited for; matrix products, arithmetic and copies ran while one was open for 0% of the time, Pallas kernels for 12%

profile of v5, /device:TPU:4, one launch (start us, length us, event | category | flops | bytes accessed | tf_op | source)
XLA Modules:
  0.0 82.1 jit_solution(14015699778546692462)
XLA Ops:
  0.0 1.5 %pack.1 = (bf16[136,256]{1,0:T(8,128)(2,1)S(1)}, bf16[136,256]{1,0:T(8,128)(2,1)S(1)}, bf16[136,256]{1,0:T(8,128)(2,1)S(1)}, bf16[136,256]{1,0:T(8,128)(2,1)S(1)...) custom-call(f32[8,16,8,256]{3,2,1,0:T(8,128)} %state_hbm.1, ...), custom_call_target="tpu_custom_call" | custom-call | bytes 1048576 | tf_op jit(solution)/shard_map/pack/pallas_call | solution.py:372
  1.5 1.9 %collective-permute-start = (bf16[136,256]{1,0:T(8,128)(2,1)S(1)}, bf16[136,256]{1,0:T(8,128)(2,1)S(1)}, u32[]{:S(2)}, u32[]{:S(2)}) collective-permute-start(bf16[136,256]{1,0:T(8,128)(2,1)S(1)} %get-tuple-element.23.lat_pair), channel_id=1, source_target_pairs={{0,16},{32,48},{64,80},{96,112},{128,144},{160,176},{192,208},{224... | collective-permute-start | bytes 208904 | tf_op jit(solution)/shard_map/ppermute | solution.py:391
  3.4 2.5 %collective-permute-start.1 = (bf16[136,256]{1,0:T(8,128)(2,1)S(1)}, bf16[136,256]{1,0:T(8,128)(2,1)S(1)}, u32[]{:S(2)}, u32[]{:S(2)}) collective-permute-start(bf16[136,256]{1,0:T(8,128)(2,1)S(1)} %get-tuple-element.24.lat_other), channel_id=1, source_target_pairs={{16,32},{48,64},{80,96},{112,128},{144,160},{176,192},{208,224},{2... | collective-permute-start | bytes 208904 | tf_op jit(solution)/shard_map/ppermute | solution.py:391
  5.9 3.6 %collective-permute-start.2 = (bf16[136,256]{1,0:T(8,128)(2,1)S(1)}, bf16[136,256]{1,0:T(8,128)(2,1)S(1)}, u32[]{:S(2)}, u32[]{:S(2)}) collective-permute-start(bf16[136,256]{1,0:T(8,128)(2,1)S(1)} %get-tuple-element.25.lev_pair), channel_id=1, source_target_pairs={{0,1},{2,3},{4,5},{6,7},{8,9},{10,11},{12,13},{14,15},{1,0},{3,2},... | collective-permute-start | bytes 208904 | tf_op jit(solution)/shard_map/ppermute | solution.py:391
  9.6 0.7 collective-permute-start.3
  10.2 0.7 interior.1.part
  11.0 0.0 collective-permute-done.from_lat_pair
  11.0 0.0 collective-permute-done.1.from_lat_other
  11.0 1.9 %collective-permute-done.2.from_lev_pair = bf16[136,256]{1,0:T(8,128)(2,1)S(1)} collective-permute-done((bf16[136,256]{1,0:T(8,128)(2,1)S(1)}, bf16[136,256]{1,0:T(8,128)(2,1)S(1)}, u32[]{:S(2)}, u32[]{:S(2)}) %collective-permute-start.2) | collective-permute-done | bytes 69664 | tf_op jit(solution)/shard_map/ppermute | solution.py:391
  12.9 0.0 collective-permute-done.3.from_lev_other
  12.9 1.3 %edges.1 = (f32[8,16,8,256]{3,2,1,0:T(8,128)S(1)}, bf16[16,16,8,128]{3,2,1,0:T(8,128)(2,1)}) custom-call(f32[8,16,8,256]{3,2,1,0:T(8,128)S(1)} %interior.1.part, bf16[136,256]{1,0:T(8,128)(2,1)S(1)} %get-tuple-element.23.lat_pair, bf16[136,256]{1,0:T(8,128)(2,1)S(1)} %get-tuple-element.24.lat_other, bf16[136,256]{1,0:T(8,128)(2,1)S(1)} %get-tuple-element.25.lev_pair, ...), custom_call_target="tpu_custom_call" | custom-call | tf_op jit(solution)/shard_map/edges/pallas_call | solution.py:408
  14.2 15.3 %all-to-all-start = ((bf16[16,16,8,128]{3,2,1,0:T(8,128)(2,1)}), bf16[16,16,8,128]{3,2,1,0:T(8,128)(2,1)S(1)}, u32[]{:S(2)}, u32[]{:S(2)}) async-start(bf16[16,16,8,128]{3,2,1,0:T(8,128)(2,1)} %get-tuple-element.28), calls=%async_computation | async-start | bytes 1048576 | tf_op jit(solution)/shard_map/all_to_all | solution.py:424
  30.1 0.0 copy-start
  30.1 0.0 copy-start.1
  30.1 9.3 %flip.1 = (bf16[768,2048]{1,0:T(8,128)(2,1)}, bf16[2048,768]{1,0:T(8,128)(2,1)}, bf16[1024,512]{1,0:T(8,128)(2,1)}, bf16[128,1024]{1,0:T(8,128)(2,1)}) custom-call(bf16[2048,768]{1,0:T(8,128)(2,1)} %in_hbm.1, bf16[768,2048]{1,0:T(8,128)(2,1)} %out_hbm.1, bf16[512,1024]{1,0:T(8,128)(2,1)} %rad_hbm.1, bf16[1024,128]{1,0:T(8,128)(2,1)} %heat_hbm.1), custom_call_target="tpu_custom_call" | custom-call | flops 4000000000 | bytes 15204352 | tf_op jit(solution)/shard_map/flip/pallas_call | solution.py:428
  39.5 10.9 %all-to-all-done.got = bf16[16,16,8,128]{3,2,1,0:T(8,128)(2,1)S(1)} async-done(((bf16[16,16,8,128]{3,2,1,0:T(8,128)(2,1)}), bf16[16,16,8,128]{3,2,1,0:T(8,128)(2,1)S(1)}, u32[]{:S(2)}, u32[]{:S(2)}) %all-to-all-start) | async-done | bytes 524320 | tf_op jit(solution)/shard_map/all_to_all | solution.py:424
  50.4 0.0 copy-done
  50.4 0.0 copy-done.1
  50.4 6.5 %columns.1 = bf16[16,16,8,128]{3,2,1,0:T(8,128)(2,1)S(1)} custom-call(s32[1,1]{1,0:T(1,128)S(6)} %copy.12.count, bf16[16,16,8,128]{3,2,1,0:T(8,128)(2,1)S(1)} %all-to-all-done.got, f32[128,128]{1,0:T(8,128)S(1)} %copy-done, bf16[768,2048]{1,0:T(8,128)(2,1)} %get-tuple-element.29.in_hbm, bf16[2048,768]{1,0:T(8,128)(2,1)} %get-tuple-element.30.out_hbm, ...), custom_call_target="tpu_custom_call" | custom-call | tf_op jit(solution)/shard_map/columns/pallas_call | solution.py:442
  56.9 24.1 %all_to_all.10.change = bf16[16,16,8,128]{3,2,1,0:T(8,128)(2,1)S(1)} all-to-all(bf16[16,16,8,128]{3,2,1,0:T(8,128)(2,1)S(1)} %columns.1), channel_id=1, replica_groups=mesh['lat'=64,'lev'=16] {'lev'}, dimensions={0} | all-to-all | bytes 1048576 | tf_op jit(solution)/shard_map/all_to_all | solution.py:460
  81.0 1.1 %finish.1 = f32[8,16,8,256]{3,2,1,0:T(8,128)} custom-call(f32[8,16,8,256]{3,2,1,0:T(8,128)S(1)} %get-tuple-element.27.moved, bf16[16,16,8,128]{3,2,1,0:T(8,128)(2,1)S(1)} %all_to_all.10.change), custom_call_target="tpu_custom_call" | custom-call | tf_op jit(solution)/shard_map/finish/pallas_call | solution.py:461
Async XLA Ops:
  1.5 9.5 %collective-permute-start = (bf16[136,256]{1,0:T(8,128)(2,1)S(1)}, bf16[136,256]{1,0:T(8,128)(2,1)S(1)}, u32[]{:S(2)}, u32[]{:S(2)}) collective-permute-start(bf16[136,256]{1,0:T(8,128)(2,1)S(1)} %get-tuple-element.23.lat_pair), channel_id=1, source_target_pairs={{0,16},{32,48},{64,80},{96,112},{128,144},{160,176},{192,208},{224... | collective-permute-start | bytes 208904 | tf_op jit(solution)/shard_map/ppermute | solution.py:391
  3.4 7.6 %collective-permute-start.1 = (bf16[136,256]{1,0:T(8,128)(2,1)S(1)}, bf16[136,256]{1,0:T(8,128)(2,1)S(1)}, u32[]{:S(2)}, u32[]{:S(2)}) collective-permute-start(bf16[136,256]{1,0:T(8,128)(2,1)S(1)} %get-tuple-element.24.lat_other), channel_id=1, source_target_pairs={{16,32},{48,64},{80,96},{112,128},{144,160},{176,192},{208,224},{2... | collective-permute-start | bytes 208904 | tf_op jit(solution)/shard_map/ppermute | solution.py:391
  5.9 6.9 %collective-permute-start.2 = (bf16[136,256]{1,0:T(8,128)(2,1)S(1)}, bf16[136,256]{1,0:T(8,128)(2,1)S(1)}, u32[]{:S(2)}, u32[]{:S(2)}) collective-permute-start(bf16[136,256]{1,0:T(8,128)(2,1)S(1)} %get-tuple-element.25.lev_pair), channel_id=1, source_target_pairs={{0,1},{2,3},{4,5},{6,7},{8,9},{10,11},{12,13},{14,15},{1,0},{3,2},... | collective-permute-start | bytes 208904 | tf_op jit(solution)/shard_map/ppermute | solution.py:391
  9.6 3.3 %collective-permute-start.3 = (bf16[136,256]{1,0:T(8,128)(2,1)S(1)}, bf16[136,256]{1,0:T(8,128)(2,1)S(1)}, u32[]{:S(2)}, u32[]{:S(2)}) collective-permute-start(bf16[136,256]{1,0:T(8,128)(2,1)S(1)} %get-tuple-element.26.lev_other), channel_id=1, source_target_pairs={{1,2},{3,4},{5,6},{7,8},{9,10},{11,12},{13,14},{2,1},{4,3},{6,5},{... | collective-permute-start | bytes 208904 | tf_op jit(solution)/shard_map/ppermute | solution.py:391
  14.2 36.2 %all-to-all-start = ((bf16[16,16,8,128]{3,2,1,0:T(8,128)(2,1)}), bf16[16,16,8,128]{3,2,1,0:T(8,128)(2,1)S(1)}, u32[]{:S(2)}, u32[]{:S(2)}) async-start(bf16[16,16,8,128]{3,2,1,0:T(8,128)(2,1)} %get-tuple-element.28), calls=%async_computation | async-start | bytes 1048576 | tf_op jit(solution)/shard_map/all_to_all | solution.py:424
  30.1 20.2 %copy-start = (f32[128,128]{1,0:T(8,128)S(1)}, f32[128,128]{1,0:T(8,128)}, u32[]{:S(2)}) copy-start(f32[128,128]{1,0:T(8,128)} %remap.1) | copy-start | bytes 196612
  30.1 20.2 %copy-start.1 = (s32[1,1,128]{2,1,0:T(1,128)S(1)}, s32[1,1,128]{2,1,0:T(1,128)}, u32[]{:S(2)}) copy-start(s32[1,1,128]{2,1,0:T(1,128)} %param.20) | copy-start | bytes 1540
